TPU v7x, 256 devices: a whole 4x4x8 slice. The times are simulated.
256 devices in a mesh: expert: 64 (over y, z, core), tensor: 4 (over x).
Axes of the slice: x: 4, y: 4, z: 8, core: 2. Of those that a mesh axis runs over, the one named last changes fastest.
Arguments:
- attn_heads: bfloat16 [8192, 4096], P('expert', 'tensor'), may hold values from -6 to 6
- out_proj: bfloat16 [4096, 4096], P('tensor', 'expert'), may hold values from -0.09375 to 0.09375
- residual: bfloat16 [8192, 4096], P('expert'), may hold values from -6 to 6
- norm_gain: float32 [4096], replicated, may hold values from 0.1 to 1.9
- route_ids: int32 [8192, 8], P('expert'), may hold values from 0 to 63, all different within a row; in each aligned block of 128 rows (0 to 127, 128 to 255, ...) at most 18 rows name the same one
- route_weights: float32 [8192, 8], P('expert'), may hold values from 0.05 to 1
- w_gate: bfloat16 [64, 4096, 1536], P('expert', None, 'tensor'), may hold values from -0.09375 to 0.09375
- w_up: bfloat16 [64, 4096, 1536], P('expert', None, 'tensor'), may hold values from -0.09375 to 0.09375
- w_down: bfloat16 [64, 1536, 4096], P('expert', 'tensor'), may hold values from -0.15625 to 0.15625
Outputs:
- layer_out: bfloat16 [8192, 4096], P('expert', 'tensor')
Inputs may be any that keep to these rules, and one draw needn't show every extreme that they name: `route_ids`: each row names 8 different experts. In aligned blocks of 128 rows no expert is named more than 18 times, a bound that some block reaches.
All inputs are finite; a program needn't handle non-finite values.
Results may differ from a plain program's by a relative error of at most 0.015.
Values may be sent and summed in bfloat16 or wider, within the bound.
A program may use at most 128 MiB of HBM per device.

v0:
```python
import jax
import jax.numpy as jnp
from jax import lax
from jax.sharding import PartitionSpec as P

EXPERTS = 64
CAP = 18


def slot_places(ids, experts, capacity):
    row_count, top_count = ids.shape
    onehot = (ids[:, :, None] == jnp.arange(experts, dtype=jnp.int32)[None, None, :]).astype(
        jnp.int32
    )
    flattened = onehot.reshape(row_count * top_count, experts)
    before = jnp.cumsum(flattened, axis=0) - flattened
    slot_rank = jnp.sum(before * flattened, axis=1).reshape(row_count, top_count)
    return ids * capacity + slot_rank


def per_device(
    attn_heads, out_proj, residual, norm_gain, route_ids, route_weights, w_gate, w_up, w_down
):
    model_width = residual.shape[1]
    groups = lax.axis_size("expert")
    members = lax.axis_size("tensor")
    member = lax.axis_index("tensor")
    per_group = w_gate.shape[0]
    slot_count = EXPERTS * CAP
    block_cols = model_width // members
    heads_out = jnp.dot(
        attn_heads,
        lax.all_gather(out_proj, "expert", axis=1, tiled=True),
        preferred_element_type=jnp.float32,
    )
    attn_out = lax.psum(heads_out.astype(jnp.bfloat16), "tensor").astype(jnp.float32)
    hidden = residual.astype(jnp.float32) + attn_out
    normed = (
        hidden * lax.rsqrt(jnp.mean(hidden * hidden, axis=-1, keepdims=True) + 1e-06) * norm_gain
    ).astype(jnp.bfloat16)
    slot_index = slot_places(route_ids, EXPERTS, CAP)
    slot_range = jnp.arange(slot_count, dtype=jnp.int32)
    slot_hits = jnp.sum(
        (slot_index[:, :, None] == slot_range[None, None, :]).astype(jnp.bfloat16), axis=1
    )
    buffer = jnp.einsum("rj,rd->jd", slot_hits, normed, preferred_element_type=jnp.float32).astype(
        jnp.bfloat16
    )
    buffer = buffer.reshape(groups, per_group, CAP, model_width)
    arrived = lax.all_to_all(buffer, "expert", split_axis=0, concat_axis=0, tiled=True)
    gate_acc = jnp.einsum("gxcd,xdf->gxcf", arrived, w_gate, preferred_element_type=jnp.float32)
    upper = jnp.einsum("gxcd,xdf->gxcf", arrived, w_up, preferred_element_type=jnp.float32)
    activation = (jax.nn.silu(gate_acc) * upper).astype(jnp.bfloat16)
    product_term = jnp.einsum(
        "gxcf,xfd->gxcd", activation, w_down, preferred_element_type=jnp.float32
    )
    product_term = lax.optimization_barrier(product_term.astype(jnp.bfloat16)).astype(jnp.float32)
    product_term = product_term.reshape(
        groups, per_group, CAP, 1 * lax.axis_size("tensor"), block_cols
    )
    shares = lax.psum_scatter(
        jnp.transpose(product_term, (3, 0, 1, 2, 4)).astype(jnp.bfloat16),
        "tensor",
        scatter_dimension=0,
        tiled=True,
    ).astype(jnp.float32)
    expert_out = shares[0].astype(jnp.bfloat16)
    returned = lax.all_to_all(expert_out, "expert", split_axis=0, concat_axis=0, tiled=True)
    weights = route_weights / jnp.sum(route_weights, axis=-1, keepdims=True)
    picked = returned.reshape(slot_count, block_cols)[slot_index]
    mixture = jnp.sum(weights[:, :, None] * picked.astype(jnp.float32), axis=1)
    own_hidden = lax.dynamic_slice_in_dim(hidden, member * block_cols, block_cols, 1)
    return (own_hidden + mixture).astype(jnp.bfloat16)


def solution(mesh):
    placed = (
        P("expert", "tensor"),
        P("tensor", "expert"),
        P("expert", None),
        P(),
        P("expert", None),
        P("expert", None),
        P("expert", None, "tensor"),
        P("expert", None, "tensor"),
        P("expert", "tensor", None),
    )
    return jax.shard_map(
        per_device, mesh=mesh, in_specs=placed, out_specs=P("expert", "tensor"), check_vma=False
    )
```

profile of v0, /device:TPU:1, one launch (start us, length us, event | category | flops | bytes accessed | tf_op | source)
XLA Modules:
  0.0 692.8 jit_solution(6831662103066266211)
XLA Ops:
  7.3 90.2 %all-gather.2.cloned.1.call-done = bf16[1024,4096]{0,1:T(8,128)(2,1)} async-done(((bf16[1024,64]{0,1:T(8,128)(2,1)}), bf16[1024,4096]{0,1:T(8,128)(2,1)}) %all-gather.2.cloned.1.call-update) | async-done | bytes 8388624 | tf_op jit(solution)/shard_map/all_gather | solution.py:33
  97.5 7.4 %convolution_convert_fusion.1 = bf16[128,4096]{1,0:T(8,128)(2,1)} fusion(bf16[128,1024]{1,0:T(8,128)(2,1)} %param.9, bf16[1024,4096]{0,1:T(8,128)(2,1)} %all-gather.2.cloned.1.call-done), kind=kOutput, calls=%fused_computation.10 | convolution fusion | flops 1074266112 | bytes 9699328 | tf_op jit(solution)/shard_map/dot_general | solution.py:31
  105.3 0.7 fusion.30
  106.0 31.1 %reduce-window.6 = s32[64,8,128]{2,1,0:T(8,128)S(1)} reduce-window(s32[64,8,128]{2,1,0:T(8,128)} %fusion.30, s32[]{:T(128)} %constant.11.clone.1), window={size=1x1x128 pad=0_0x0_0x127_0}, to_apply=%region_2.0 | reduce-window | flops 8323072 | bytes 524292 | tf_op jit(solution)/shard_map/reduce-window
  137.1 0.8 slice.10
  138.0 1.1 copy.49
  139.7 1.5 fusion.11
  141.1 10.4 %all-reduce.2.cloned.1.call-done = bf16[128,4096]{1,0:T(8,128)(2,1)} async-done(((bf16[128,4096]{1,0:T(8,128)(2,1)}), bf16[128,4096]{1,0:T(8,128)(2,1)}) %all-reduce.2.cloned.1.call-update) | async-done | bytes 1048592 | tf_op jit(solution)/shard_map/psum | solution.py:36
  151.5 3.4 convert_add_fusion
  155.0 5.1 convolution_convert_fusion
  160.1 13.9 %reshape.76 = bf16[64,1,18,4096]{3,2,0,1:T(8,128)(2,1)} reshape(bf16[1152,4096]{1,0:T(8,128)(2,1)} %convolution_convert_fusion) | data formatting | bytes 18874368 | tf_op jit(solution)/shard_map/reshape | solution.py:49
  174.0 288.3 %all_to_all.10 = bf16[64,1,18,4096]{3,2,1,0:T(8,128)(2,1)S(1)} all-to-all(bf16[64,1,18,4096]{3,2,1,0:T(8,128)(2,1)} %bitcast.96), channel_id=1, replica_groups=mesh['expert'=64,'tensor'=4] {'expert'}, dimensions={0} | all-to-all | bytes 18874368 | tf_op jit(solution)/shard_map/all_to_all | solution.py:50
  462.3 6.2 fusion.2
  468.5 7.3 %fusion.20 = bf16[64,18,384]{2,0,1:T(8,128)(2,1)S(1)} fusion(bf16[1,4096,384]{2,1,0:T(8,128)(2,1)S(1)} %copy-done.7, bf16[64,1,18,4096]{3,2,1,0:T(8,128)(2,1)S(1)} %all_to_all.10, f32[64,18,384]{2,0,1:T(8,128)S(1)} %fusion.2), kind=kOutput, calls=%fused_computation.29 | convolution fusion | flops 3626532864 | bytes 15237120 | tf_op jit(solution)/shard_map/gxcd,xdf->gxcf/dot_general | solution.py:52
  475.9 7.5 %convert_bitcast_fusion = bf16[64,1,18,4096]{3,0,2,1:T(8,128)(2,1)} fusion(bf16[64,18,384]{2,0,1:T(8,128)(2,1)S(1)} %fusion.20, bf16[1,384,4096]{2,1,0:T(8,128)(2,1)S(1)} %copy-done), kind=kOutput, calls=%fused_computation.7 | convolution fusion | flops 3628597248 | bytes 13467648 | tf_op jit(solution)/shard_map/gxcf,xfd->gxcd/dot_general | solution.py:54
  483.3 9.0 %copy.74 = bf16[1,18,8,4,8,1024]{5,4,2,1,0,3:T(8,128)(2,1)} copy(bf16[1,18,8,4,8,1024]{5,4,3,2,1,0:T(8,128)(2,1)} %bitcast.98) | data formatting | bytes 18874368 | tf_op jit(solution)/shard_map/convert_element_type | solution.py:62
  492.3 87.7 %reduce-scatter.2.cloned.1.call-done = bf16[1,64,1,18,1024]{4,1,3,2,0:T(8,128)(2,1)} async-done(((bf16[4,64,1,18,1024]{4,1,3,2,0:T(8,128)(2,1)}), bf16[1,64,1,18,1024]{4,1,3,2,0:T(8,128)(2,1)}) %reduce-scatter.2.cloned.1.call-update) | async-done | bytes 2359312 | tf_op jit(solution)/shard_map/reduce_scatter | solution.py:61
  580.1 4.7 copy.56
  584.8 10.9 %all-to-all-start.1 = ((bf16[64,1,18,1024]{3,2,1,0:T(8,128)(2,1)}), bf16[64,1,18,1024]{3,2,1,0:T(8,128)(2,1)}, u32[]{:S(2)}, u32[]{:S(2)}) async-start(bf16[64,1,18,1024]{3,2,1,0:T(8,128)(2,1)} %copy.56), calls=%async_computation.2 | async-start | bytes 6291456 | tf_op jit(solution)/shard_map/all_to_all | solution.py:68
  596.1 73.1 %all-to-all-done.1 = bf16[64,1,18,1024]{3,2,1,0:T(8,128)(2,1)} async-done(((bf16[64,1,18,1024]{3,2,1,0:T(8,128)(2,1)}), bf16[64,1,18,1024]{3,2,1,0:T(8,128)(2,1)}, u32[]{:S(2)}, u32[]{:S(2)}) %all-to-all-start.1) | async-done | bytes 2359328 | tf_op jit(solution)/shard_map/all_to_all | solution.py:68
  669.2 4.3 reshape.82
  673.5 8.0 %gather_fusion = bf16[1024,1024]{1,0:T(8,128)(2,1)} fusion(bf16[1152,1024]{1,0:T(8,128)(2,1)} %reshape.82, s32[1024]{0:T(1024)S(1)} %broadcast_clamp_fusion), kind=kCustom, calls=%fused_computation | custom fusion | bytes 4198400 | tf_op jit(solution)/shard_map/gather | solution.py:70
  681.5 2.9 fusion.7
  684.4 1.8 add_convert_fusion
  (41 shorter events, 2.0 us)
Async XLA Ops:
  6.5 469.3 %copy-start = (bf16[1,384,4096]{2,1,0:T(8,128)(2,1)S(1)}, bf16[1,384,4096]{2,1,0:T(8,128)(2,1)}, u32[]{:S(2)}) copy-start(bf16[1,384,4096]{2,1,0:T(8,128)(2,1)} %param.17) | copy-start | bytes 9437188
  6.5 90.9 %all-gather.2.cloned.1.call-start = ((), (), s32[]{:S(2)}) async-start(), calls=%async_computation.3 | async-start | bytes 8519680 | tf_op jit(solution)/shard_map/all_gather | solution.py:33
  7.3 97.7 %copy-start.4 = (s32[128,8]{0,1:T(8,128)S(1)}, s32[128,8]{0,1:T(8,128)}, u32[]{:S(2)}) copy-start(s32[128,8]{0,1:T(8,128)} %param.13) | copy-start | bytes 12292
  7.3 144.2 %all-reduce.2.cloned.1.call-start = ((), (), s32[]{:S(2)}) async-start(), calls=%async_computation.4 | async-start | bytes 2097152 | tf_op jit(solution)/shard_map/psum | solution.py:36
  104.9 475.1 %reduce-scatter.2.cloned.1.call-start = ((), (), s32[]{:S(2)}) async-start(), calls=%async_computation.5 | async-start | bytes 11796480 | tf_op jit(solution)/shard_map/reduce_scatter | solution.py:61
  137.1 17.8 %copy-start.5 = (f32[4096]{0:T(1024)S(1)}, f32[4096]{0:T(1024)}, u32[]{:S(2)}) copy-start(f32[4096]{0:T(1024)} %param.12) | copy-start | bytes 49156
  151.5 3.4 copy-start.1
  151.5 3.4 copy-start.2
  174.0 288.3 %copy-start.6 = (bf16[1,4096,384]{2,1,0:T(8,128)(2,1)S(1)}, bf16[1,4096,384]{2,1,0:T(8,128)(2,1)}, u32[]{:S(2)}) copy-start(bf16[1,4096,384]{2,1,0:T(8,128)(2,1)} %param.15) | copy-start | bytes 9437188
  462.3 6.2 copy-start.7
  584.8 11.2 %copy-start.3 = (f32[128,8]{0,1:T(8,128)S(1)}, f32[128,8]{0,1:T(8,128)}, u32[]{:S(2)}) copy-start(f32[128,8]{0,1:T(8,128)} %param.14) | copy-start | bytes 12292
  584.8 84.4 %all-to-all-start.1 = ((bf16[64,1,18,1024]{3,2,1,0:T(8,128)(2,1)}), bf16[64,1,18,1024]{3,2,1,0:T(8,128)(2,1)}, u32[]{:S(2)}, u32[]{:S(2)}) async-start(bf16[64,1,18,1024]{3,2,1,0:T(8,128)(2,1)} %copy.56), calls=%async_computation.2 | async-start | bytes 6291456 | tf_op jit(solution)/shard_map/all_to_all | solution.py:68
Sparse Core Ops, SparseCore 0:
  10.1 87.2 all-gather.1
  105.1 46.4 all-reduce.1
  492.4 87.5 reduce-scatter.1
where the time goes:
time: 695 us; the launch traced here: 693 us
  blocking collectives  288 us (41%)
  waiting for transfers between devices  262 us (38%)
  local copies, waits for them, and re-layouts  42.8 us (6%)
  other arithmetic  41.7 us (6%)
  matrix products  33.6 us (5%)
  between operations  13.3 us (2%)
  starting transfers between devices  11 us (2%)
    all_to_all x1, blocking collectives, per_device(): lax.all_to_all(buffer, 'expert', split_axis=0, concat_axis=0, tiled=True)  288 us
    all_gather x1, waiting for transfers between devices, per_device(): lax.all_gather(out_proj, 'expert', axis=1, tiled=True)  90.2 us
    reduce_scatter x1, waiting for transfers between devices, per_device(): lax.psum_scatter(jnp.transpose(product_term, (3, 0, 1, 2, 4)).astype(jnp....  87.7 us
    all_to_all x1, waiting for transfers between devices, per_device(): lax.all_to_all(expert_out, 'expert', split_axis=0, concat_axis=0, tiled=T...  73.1 us
    another operation x3, other arithmetic  31.3 us
    reshape x1, local copies, waits for them, and re-layouts, per_device(): buffer = buffer.reshape(groups, per_group, CAP, model_width)  13.9 us
  transfers between devices with their start and end apart: 4, of which 4 were waited for; matrix products, arithmetic and copies ran while one was open for 5% of the time, Pallas kernels for 0%

commit v1 on v0

v1 whole, which is shorter than its diff:
```python
import jax
import jax.numpy as jnp
from jax import lax
from jax.sharding import PartitionSpec as P

EXPERTS = 64
MAIN = 16
OVER = 2
LANES = 128


def routing(route_ids, route_weights):
    count = route_ids.shape[0]
    hits = (route_ids[:, :, None] == jnp.arange(EXPERTS, dtype=jnp.int32)[None, None, :]).astype(
        jnp.float32
    )
    chosen = jnp.sum(hits, axis=1)
    weights = route_weights / jnp.sum(route_weights, axis=-1, keepdims=True)
    weight = jnp.sum(hits * weights[:, :, None], axis=1)
    order = jnp.arange(count, dtype=jnp.int32)
    earlier = (order[None, :] < order[:, None]).astype(jnp.bfloat16)
    rank = jnp.dot(earlier, chosen.astype(jnp.bfloat16), preferred_element_type=jnp.float32)
    rank = jnp.where(chosen > 0, rank, -1.0)
    return rank.astype(jnp.int32), weight


def per_device(
    attn_heads, out_proj, residual, norm_gain, route_ids, route_weights, w_gate, w_up, w_down
):
    tokens, model_width = residual.shape
    members = lax.axis_size("tensor")
    member = lax.axis_index("tensor")
    cols = model_width // members
    groups = cols // LANES
    rows = EXPERTS * MAIN

    rank, weight = routing(route_ids, route_weights)
    row = jnp.arange(rows, dtype=jnp.int32)
    slot = row % MAIN
    spread = jnp.repeat(rank, MAIN, axis=1)
    main_hit = spread == slot[None, :]
    over_hit = spread == (MAIN + slot // groups)[None, :]
    row_weight = jnp.repeat(weight, MAIN, axis=1)

    heads_out = jnp.dot(
        attn_heads,
        lax.all_gather(out_proj, "expert", axis=1, tiled=True),
        preferred_element_type=jnp.float32,
    ).astype(jnp.bfloat16)
    attn_out = lax.psum_scatter(
        jnp.transpose(heads_out.reshape(tokens, members, cols), (1, 0, 2)),
        "tensor",
        scatter_dimension=0,
        tiled=True,
    )[0].astype(jnp.float32)
    own_residual = lax.dynamic_slice_in_dim(residual, member * cols, cols, 1)
    own_gain = lax.dynamic_slice_in_dim(norm_gain, member * cols, cols, 0)
    hidden = own_residual.astype(jnp.float32) + attn_out
    squares = lax.psum(jnp.sum(hidden * hidden, axis=-1, keepdims=True), "tensor")
    normed = (hidden * lax.rsqrt(squares / model_width + 1e-06) * own_gain).astype(jnp.bfloat16)

    main = jnp.einsum(
        "tr,td->rd", main_hit.astype(jnp.bfloat16), normed, preferred_element_type=jnp.float32
    ).astype(jnp.bfloat16)
    wide = jnp.einsum(
        "tr,td->rd", over_hit.astype(jnp.bfloat16), normed, preferred_element_type=jnp.float32
    ).astype(jnp.bfloat16)
    own_group = (row % groups)[:, None]
    over = jnp.zeros((rows, LANES), jnp.bfloat16)
    for g in range(groups):
        over = jnp.where(own_group == g, wide[:, g * LANES : (g + 1) * LANES], over)
    packed = jnp.concatenate([main, over], axis=1).reshape(EXPERTS, MAIN, cols + LANES)
    arrived = lax.all_to_all(packed, "expert", split_axis=0, concat_axis=0, tiled=True)
    full = lax.all_gather(arrived.reshape(rows, cols + LANES), "tensor", axis=0)
    main_in = jnp.concatenate([full[m, :, :cols] for m in range(members)], axis=1)
    over_in = jnp.transpose(
        full[:, :, cols:].reshape(members, EXPERTS * OVER, groups, LANES), (1, 0, 2, 3)
    ).reshape(EXPERTS * OVER, model_width)
    inputs = jnp.concatenate([main_in, over_in], axis=0)
    gate = jnp.dot(inputs, w_gate[0], preferred_element_type=jnp.float32)
    up = jnp.dot(inputs, w_up[0], preferred_element_type=jnp.float32)
    act = (jax.nn.silu(gate) * up).astype(jnp.bfloat16)
    down = w_down[0].reshape(-1, members, cols)
    parts = jnp.stack(
        [jnp.dot(act, down[:, m], preferred_element_type=jnp.float32) for m in range(members)]
    ).astype(jnp.bfloat16)
    summed = lax.psum_scatter(parts, "tensor", scatter_dimension=0, tiled=True)[0]
    back = jnp.concatenate(
        [summed[:rows], summed[rows:].reshape(rows, LANES)], axis=1
    ).reshape(EXPERTS, MAIN, cols + LANES)
    returned = lax.all_to_all(back, "expert", split_axis=0, concat_axis=0, tiled=True).reshape(
        rows, cols + LANES
    )
    high = row_weight.astype(jnp.bfloat16)
    low = (row_weight - high.astype(jnp.float32)).astype(jnp.bfloat16)
    mixture = 0.0
    zero = jnp.zeros((), jnp.bfloat16)
    for part in (high, low):
        pick = jnp.where(main_hit, part, zero)
        mixture += jnp.dot(pick, returned[:, :cols], preferred_element_type=jnp.float32)
        extra = [
            jnp.dot(
                jnp.where(over_hit & (row % groups == g)[None, :], part, zero),
                returned[:, cols:],
                preferred_element_type=jnp.float32,
            )
            for g in range(groups)
        ]
        mixture += jnp.concatenate(extra, axis=1)
    return (hidden + mixture).astype(jnp.bfloat16)


def solution(mesh):
    placed = (
        P("expert", "tensor"),
        P("tensor", "expert"),
        P("expert", None),
        P(),
        P("expert", None),
        P("expert", None),
        P("expert", None, "tensor"),
        P("expert", None, "tensor"),
        P("expert", "tensor", None),
    )
    return jax.shard_map(
        per_device, mesh=mesh, in_specs=placed, out_specs=P("expert", "tensor"), check_vma=False
    )
```

time: 695 us -> 546 us (0.79)
  blocking collectives: 288 us -> 77.7 us
  waiting for transfers between devices: 262 us -> 336 us
  matrix products: 33.6 us -> 62.3 us
  other arithmetic: 41.7 us -> 18.2 us
  local copies, waits for them, and re-layouts: 42.8 us -> 26.1 us
    all_to_all x1, blocking collectives: 288 us -> 71.2 us  [per_device(): lax.all_to_all(packed, 'expert', split_axis=0, concat_axis=0, tiled=True)]
    all_gather x0 -> x1, waiting for transfers between devices: none -> 84.6 us  [per_device(): full = lax.all_gather(arrived.reshape(rows, cols + LANES), 'tensor', axis=0)]
    dot_general x4 -> x27, matrix products: 26.2 us -> 56 us  [the longest x1 19.2 us: per_device(): gate = jnp.dot(inputs, w_gate[0], preferred_element_type=jnp.float32)]
    another operation x3 -> x1, other arithmetic: 31.3 us -> 4.56 us  [per_device(): jnp.stack([jnp.dot(act, down[:, m], preferred_element_type=jnp.float32) f...]
    all_to_all x1, waiting for transfers between devices: 73.1 us -> 51.9 us  [per_device(): lax.all_to_all(back, 'expert', split_axis=0, concat_axis=0, tiled=True)]
    reduce_scatter x1 -> x2, waiting for transfers between devices: 87.7 us -> 108 us  [the longest x1 92.7 us: per_device(): lax.psum_scatter(parts, 'tensor', scatter_dimension=0, tiled=True)[0]]
    reshape x4 -> x2, local copies, waits for them, and re-layouts: 18.4 us -> 3.38 us  [the longest x1 2.31 us: per_device(): over_in = jnp.transpose(full[:, :, cols:].reshape(members, EXPERTS * OVER...]
    convert_element_type x2 -> x0, local copies, waits for them, and re-layouts: 13.7 us -> none  [the longest x1 8.95 us: per_device(): jnp.transpose(product_term, (3, 0, 1, 2, 4)).astype(jnp.bfloat16)]
  transfers between devices with their start and end apart: 4 -> 5, of which waited for: 4 -> 5; matrix products, arithmetic and copies ran while one was open for 5% -> 3% of each run, Pallas kernels for 0% -> 0%
where the time goes in v1:
time: 546 us; the launch traced here: 545 us
  waiting for transfers between devices  336 us (62%)
  blocking collectives  77.7 us (14%)
  matrix products  62.3 us (11%)
  local copies, waits for them, and re-layouts  26.1 us (5%)
  other arithmetic  18.2 us (3%)
  between operations  13.9 us (3%)
  starting transfers between devices  11 us (2%)
    reduce_scatter x1, waiting for transfers between devices, per_device(): lax.psum_scatter(parts, 'tensor', scatter_dimension=0, tiled=True)[0]  92.7 us
    all_gather x1, waiting for transfers between devices, per_device(): lax.all_gather(out_proj, 'expert', axis=1, tiled=True)  90.1 us
    all_gather x1, waiting for transfers between devices, per_device(): full = lax.all_gather(arrived.reshape(rows, cols + LANES), 'tensor', axis=0)  84.6 us
    all_to_all x1, blocking collectives, per_device(): lax.all_to_all(packed, 'expert', split_axis=0, concat_axis=0, tiled=True)  71.2 us
    all_to_all x1, waiting for transfers between devices, per_device(): lax.all_to_all(back, 'expert', split_axis=0, concat_axis=0, tiled=True)  51.9 us
    dot_general x1, matrix products, per_device(): gate = jnp.dot(inputs, w_gate[0], preferred_element_type=jnp.float32)  19.2 us
    dot_general x1, matrix products, per_device(): up = jnp.dot(inputs, w_up[0], preferred_element_type=jnp.float32)  16.9 us
    reduce_scatter x1, waiting for transfers between devices, per_device(): lax.psum_scatter(jnp.transpose(heads_out.reshape(tokens, members, cols),...  15.7 us
  transfers between devices with their start and end apart: 5, of which 5 were waited for; matrix products, arithmetic and copies ran while one was open for 3% of the time, Pallas kernels for 0%

profile of v1, /device:TPU:1, one launch (start us, length us, event | category | flops | bytes accessed | tf_op | source)
XLA Modules:
  0.0 545.0 jit_solution(5907444600638670567)
XLA Ops:
  7.3 90.1 %all-gather.3.cloned.1.call-done = bf16[1024,4096]{0,1:T(8,128)(2,1)} async-done(((bf16[1024,64]{0,1:T(8,128)(2,1)}), bf16[1024,4096]{0,1:T(8,128)(2,1)}) %all-gather.3.cloned.1.call-update) | async-done | bytes 8388624 | tf_op jit(solution)/shard_map/all_gather | solution.py:47
  97.5 6.3 %convolution_convert_fusion = bf16[128,4096]{1,0:T(8,128)(2,1)S(1)} fusion(bf16[128,1024]{1,0:T(8,128)(2,1)} %param.9, bf16[1024,4096]{0,1:T(8,128)(2,1)} %all-gather.3.cloned.1.call-done), kind=kOutput, calls=%fused_computation.2 | convolution fusion | flops 1074266112 | bytes 9699328 | tf_op jit(solution)/shard_map/dot_general | solution.py:45
  110.8 15.7 %reduce-scatter.3.cloned.1.call-done = bf16[1,128,1024]{2,1,0:T(8,128)(2,1)} async-done(((bf16[4,128,1024]{2,1,0:T(8,128)(2,1)}), bf16[1,128,1024]{2,1,0:T(8,128)(2,1)}) %reduce-scatter.3.cloned.1.call-update) | async-done | bytes 262160 | tf_op jit(solution)/shard_map/reduce_scatter | solution.py:50
  127.7 6.5 %psum.7 = f32[128,1]{0,1:T(1,128)S(1)} all-reduce(f32[128,1]{0,1:T(1,128)S(1)} %bitcast.221), channel_id=1, replica_groups=mesh['expert'=64,'tensor'=4] {'tensor'}, use_global_device_ids=true, to_apply=%region_5.6 | all-reduce | flops 128 | bytes 1024 | tf_op jit(solution)/shard_map/psum | solution.py:59
  134.3 2.0 convolution_convert_fusion.5
  136.6 1.8 convolution_convert_fusion.6
  140.0 4.4 copy.131
  144.3 71.2 %all_to_all.10 = bf16[64,16,1152]{2,1,0:T(8,128)(2,1)} all-to-all(bf16[64,16,1152]{2,1,0:T(8,128)(2,1)} %bitcast.212), channel_id=1, replica_groups=mesh['expert'=64,'tensor'=4] {'expert'}, dimensions={0} | all-to-all | bytes 4718592 | tf_op jit(solution)/shard_map/all_to_all | solution.py:73
  215.8 4.7 copy.134
  220.5 84.6 %all-gather.5.cloned.1.call-done = bf16[4,1024,1152]{2,1,0:T(8,128)(2,1)} async-done(((bf16[1,1024,1152]{2,1,0:T(8,128)(2,1)}), bf16[4,1024,1152]{2,1,0:T(8,128)(2,1)}) %all-gather.5.cloned.1.call-update) | async-done | bytes 9437200 | tf_op jit(solution)/shard_map/all_gather | solution.py:74
  305.1 2.3 slice_bitcast_fusion.4
  307.3 2.4 copy.132
  309.8 2.3 copy.133
  312.1 4.9 slice_bitcast_fusion.3
  317.0 19.2 %fusion.5 = f32[1152,384]{1,0:T(8,128)} fusion(bf16[1,4096,384]{2,1,0:T(8,128)(2,1)S(1)} %copy-done, bf16[128,4096]{1,0:T(8,128)(2,1)S(1)} %copy-done.19, bf16[1024,1024]{1,0:T(8,128)(2,1)S(1)} %get-tuple-element.8, bf16[1024,1024]{1,0:T(8,128)(2,1)S(1)} %get-tuple-element.9, bf16[1024,1024]{1,0:T(8,128)(2,1)} %get-tuple-element.10, ...), kind=kOutput, calls=%fused_computation.13 | convolution fusion | flops 3671064576 | bytes 14352384 | tf_op jit(solution)/shard_map/dot_general | solution.py:80
  336.3 16.9 %fusion.7 = bf16[1152,384]{1,0:T(8,128)(2,1)} fusion(bf16[1,4096,384]{2,1,0:T(8,128)(2,1)} %param.16, f32[1152,384]{1,0:T(8,128)} %fusion.5, bf16[128,4096]{1,0:T(8,128)(2,1)S(1)} %copy-done.19, bf16[1024,1024]{1,0:T(8,128)(2,1)S(1)} %get-tuple-element.8, bf16[1024,1024]{1,0:T(8,128)(2,1)S(1)} %get-tuple-element.9, ...), kind=kOutput, calls=%fused_computation.15 | convolution fusion | flops 3673718784 | bytes 15237120 | tf_op jit(solution)/shard_map/dot_general | solution.py:81
  353.2 2.7 fusion.3
  360.1 4.6 pad_maximum_fusion.1
  364.7 92.7 %reduce-scatter.5.cloned.1.call-done = bf16[1,1152,1024]{2,1,0:T(8,128)(2,1)} async-done(((bf16[4,1152,1024]{2,1,0:T(8,128)(2,1)}), bf16[1,1152,1024]{2,1,0:T(8,128)(2,1)}) %reduce-scatter.5.cloned.1.call-update) | async-done | bytes 2359312 | tf_op jit(solution)/shard_map/reduce_scatter | solution.py:87
  461.7 10.6 %all-to-all-start.1 = ((bf16[64,16,1152]{2,1,0:T(8,128)(2,1)}), bf16[64,16,1152]{2,1,0:T(8,128)(2,1)S(1)}, u32[]{:S(2)}, u32[]{:S(2)}) async-start(bf16[64,16,1152]{2,1,0:T(8,128)(2,1)} %pad_maximum_fusion.3), calls=%async_computation.3 | async-start | bytes 4718592 | tf_op jit(solution)/shard_map/all_to_all | solution.py:91
  472.5 4.6 fusion.39
  477.1 51.9 %all-to-all-done.1 = bf16[64,16,1152]{2,1,0:T(8,128)(2,1)S(1)} async-done(((bf16[64,16,1152]{2,1,0:T(8,128)(2,1)}), bf16[64,16,1152]{2,1,0:T(8,128)(2,1)S(1)}, u32[]{:S(2)}, u32[]{:S(2)}) %all-to-all-start.1) | async-done | bytes 2359328 | tf_op jit(solution)/shard_map/all_to_all | solution.py:91
  529.1 1.7 fusion.10
  535.5 3.0 fusion.26
  (128 shorter events, 23.9 us)
Async XLA Ops:
  6.5 310.5 %copy-start = (bf16[1,4096,384]{2,1,0:T(8,128)(2,1)S(1)}, bf16[1,4096,384]{2,1,0:T(8,128)(2,1)}, u32[]{:S(2)}) copy-start(bf16[1,4096,384]{2,1,0:T(8,128)(2,1)} %param.15) | copy-start | bytes 9437188
  6.5 90.9 %all-gather.3.cloned.1.call-start = ((), (), s32[]{:S(2)}) async-start(), calls=%async_computation.4 | async-start | bytes 8519680 | tf_op jit(solution)/shard_map/all_gather | solution.py:47
  7.3 119.3 %reduce-scatter.3.cloned.1.call-start = ((), (), s32[]{:S(2)}) async-start(), calls=%async_computation.5 | async-start | bytes 1310720 | tf_op jit(solution)/shard_map/reduce_scatter | solution.py:50
  104.9 200.2 %all-gather.5.cloned.1.call-start = ((), (), s32[]{:S(2)}) async-start(), calls=%async_computation.6 | async-start | bytes 11796480 | tf_op jit(solution)/shard_map/all_gather | solution.py:74
  215.5 241.9 %reduce-scatter.5.cloned.1.call-start = ((), (), s32[]{:S(2)}) async-start(), calls=%async_computation.7 | async-start | bytes 11796480 | tf_op jit(solution)/shard_map/reduce_scatter | solution.py:87
  312.1 5.0 copy-start.19
  336.3 16.9 %copy-start.4 = (bf16[1,384,4096]{1,2,0:T(8,128)(2,1)S(1)}, bf16[1,384,4096]{1,2,0:T(8,128)(2,1)}, u32[]{:S(2)}) copy-start(bf16[1,384,4096]{1,2,0:T(8,128)(2,1)} %copy.134) | copy-start | bytes 9437188
  353.1 2.7 copy-start.39
  461.7 10.7 %copy-start.20 = (f32[128,64]{0,1:T(8,128)S(1)}, f32[128,64]{0,1:T(8,128)}, u32[]{:S(2)}) copy-start(f32[128,64]{0,1:T(8,128)} %get-tuple-element.6) | copy-start | bytes 98308
  461.7 10.7 %copy-start.22 = (s32[128,64]{0,1:T(8,128)S(1)}, s32[128,64]{0,1:T(8,128)}, u32[]{:S(2)}) copy-start(s32[128,64]{0,1:T(8,128)} %copy-done.21) | copy-start | bytes 98308
  461.7 10.7 %copy-start.25 = (pred[1024]{0:T(1024)(128)(4,1)S(1)}, pred[1024]{0:T(1024)(128)(4,1)}, u32[]{:S(2)}) copy-start(pred[1024]{0:T(1024)(128)(4,1)} %get-tuple-element.70) | copy-start | bytes 3076
  461.7 10.7 %copy-start.27 = (pred[1024]{0:T(1024)(128)(4,1)S(1)}, pred[1024]{0:T(1024)(128)(4,1)}, u32[]{:S(2)}) copy-start(pred[1024]{0:T(1024)(128)(4,1)} %get-tuple-element.67) | copy-start | bytes 3076
  461.7 10.7 %copy-start.29 = (pred[1024]{0:T(1024)(128)(4,1)S(1)}, pred[1024]{0:T(1024)(128)(4,1)}, u32[]{:S(2)}) copy-start(pred[1024]{0:T(1024)(128)(4,1)} %get-tuple-element.68) | copy-start | bytes 3076
  461.7 10.7 %copy-start.31 = (pred[1024]{0:T(1024)(128)(4,1)S(1)}, pred[1024]{0:T(1024)(128)(4,1)}, u32[]{:S(2)}) copy-start(pred[1024]{0:T(1024)(128)(4,1)} %get-tuple-element.65) | copy-start | bytes 3076
  461.7 10.7 %copy-start.33 = (pred[1024]{0:T(1024)(128)(4,1)S(1)}, pred[1024]{0:T(1024)(128)(4,1)}, u32[]{:S(2)}) copy-start(pred[1024]{0:T(1024)(128)(4,1)} %get-tuple-element.66) | copy-start | bytes 3076
  461.7 10.7 %copy-start.35 = (pred[1024]{0:T(1024)(128)(4,1)S(1)}, pred[1024]{0:T(1024)(128)(4,1)}, u32[]{:S(2)}) copy-start(pred[1024]{0:T(1024)(128)(4,1)} %get-tuple-element.63) | copy-start | bytes 3076
  461.7 10.7 %copy-start.37 = (pred[1024]{0:T(1024)(128)(4,1)S(1)}, pred[1024]{0:T(1024)(128)(4,1)}, u32[]{:S(2)}) copy-start(pred[1024]{0:T(1024)(128)(4,1)} %get-tuple-element.64) | copy-start | bytes 3076
  461.7 67.3 %all-to-all-start.1 = ((bf16[64,16,1152]{2,1,0:T(8,128)(2,1)}), bf16[64,16,1152]{2,1,0:T(8,128)(2,1)S(1)}, u32[]{:S(2)}, u32[]{:S(2)}) async-start(bf16[64,16,1152]{2,1,0:T(8,128)(2,1)} %pad_maximum_fusion.3), calls=%async_computation.3 | async-start | bytes 4718592 | tf_op jit(solution)/shard_map/all_to_all | solution.py:91
  529.0 6.1 %copy-start.2 = (bf16[64,16,1152]{2,1,0:T(8,128)(2,1)}, bf16[64,16,1152]{2,1,0:T(8,128)(2,1)S(1)}, u32[]{:S(2)}) copy-start(bf16[64,16,1152]{2,1,0:T(8,128)(2,1)S(1)} %all-to-all-done.1) | copy-start | bytes 7077892
  529.0 2.4 copy-start.16
  529.1 2.7 copy-start.15
  529.1 3.0 copy-start.14
  529.1 3.3 copy-start.13
  535.5 3.0 copy-start.1
  (22 other events, 43.5 us)
Sparse Core Ops, SparseCore 0:
  10.1 87.2 all-gather.2
  105.0 21.4 reduce-scatter.2
  215.7 89.3 all-gather.4
  364.8 92.5 reduce-scatter.4

commit v2 on v1

--- a/solution.py
+++ b/solution.py
@@ -1,17 +1,30 @@
 import jax
 import jax.numpy as jnp
+import numpy as np
 from jax import lax
+from jax.experimental import pallas as pl
+from jax.experimental.pallas import tpu as pltpu
 from jax.sharding import PartitionSpec as P
 
+MESH = pl.DeviceIdType.MESH
 EXPERTS = 64
+RING = 16
+ROWS_Y = EXPERTS // RING
 MAIN = 16
 OVER = 2
 LANES = 128
-
-
-def routing(route_ids, route_weights):
-    count = route_ids.shape[0]
-    hits = (route_ids[:, :, None] == jnp.arange(EXPERTS, dtype=jnp.int32)[None, None, :]).astype(
+CHUNKS = 4
+PER = EXPERTS // CHUNKS
+CHUNK_MAIN = PER * MAIN
+CHUNK_OVER = PER * OVER
+CHUNK_ROWS = CHUNK_MAIN + CHUNK_OVER
+HALF_IN = CHUNK_MAIN // 2
+HALF_OUT = CHUNK_ROWS // 2 // 16 * 16
+
+
+def routing(ids, route_weights):
+    count = ids.shape[0]
+    hits = (ids[:, :, None] == jnp.arange(EXPERTS, dtype=jnp.int32)[None, None, :]).astype(
         jnp.float32
     )
     chosen = jnp.sum(hits, axis=1)
@@ -24,17 +37,310 @@
     return rank.astype(jnp.int32), weight
 
 
+def overflow_order():
+    groups = MAIN // OVER
+    matrix = np.zeros((CHUNK_MAIN, CHUNK_MAIN), np.float32)
+    for g in range(groups):
+        for s in range(PER):
+            for c in range(OVER):
+                matrix[g * CHUNK_OVER + s * OVER + c, s * MAIN + c * groups + g] = 1.0
+    return matrix
+
+
+def expert_kernel(
+    packed, gate_hbm, up_hbm, down_hbm, sort, unsort, back,
+    inbox, gate_up, down, acc, to_right, to_left, to_far, own,
+    far_a, far_b, from_left, from_right, outbox,
+    weight_sem, local_sem, dsend, drecv, asend, arecv, rsend, rrecv, bsend, brecv,
+):
+    me = lax.axis_index("expert")
+    x = lax.axis_index("tensor")
+    y, zc = lax.div(me, RING), lax.rem(me, RING)
+    right, left, far = lax.rem(x + 1, 4), lax.rem(x + 3, 4), lax.rem(x + 2, 4)
+    ff = gate_hbm.shape[1]
+    cols = packed.shape[1] - LANES
+    groups = cols // LANES
+
+    def ahead(k):
+        return lax.rem(y + lax.div(k, RING), ROWS_Y) * RING + lax.rem(zc + lax.rem(k, RING), RING)
+
+    def behind(k):
+        return lax.rem(y + ROWS_Y - lax.div(k, RING), ROWS_Y) * RING + lax.rem(
+            zc + RING - lax.rem(k, RING), RING
+        )
+
+    weights = [
+        pltpu.make_async_copy(gate_hbm, gate_up.at[:, pl.ds(0, ff)], weight_sem.at[0]),
+        pltpu.make_async_copy(up_hbm, gate_up.at[:, pl.ds(ff, ff)], weight_sem.at[1]),
+        pltpu.make_async_copy(down_hbm, down, weight_sem.at[2]),
+    ]
+    for copy in weights:
+        copy.start()
+
+    barrier = pltpu.get_barrier_semaphore()
+
+    @pl.loop(1, EXPERTS)
+    def _(k):
+        pl.semaphore_signal(barrier, inc=1, device_id=(ahead(k), x), device_id_type=MESH)
+
+    for m in (right, left):
+        pl.semaphore_signal(barrier, inc=1, device_id=(me, m), device_id_type=MESH)
+    pl.semaphore_wait(barrier, EXPERTS + 1)
+
+    def block(k):
+        return pl.ds(pl.multiple_of(k * MAIN, MAIN), MAIN)
+
+    def dispatch(k):
+        return pltpu.make_async_remote_copy(
+            src_ref=packed.at[block(k)],
+            dst_ref=inbox.at[lax.div(k, PER), x, block(lax.rem(k, PER))],
+            send_sem=dsend.at[k],
+            recv_sem=drecv.at[k],
+            device_id=(ahead(k), x),
+            device_id_type=MESH,
+        )
+
+    own_in = pltpu.make_async_copy(
+        packed.at[pl.ds(0, MAIN)], inbox.at[0, x, pl.ds(0, MAIN)], local_sem.at[0]
+    )
+    own_in.start()
+
+    @pl.loop(1, EXPERTS)
+    def _(k):
+        dispatch(k).start()
+
+    own_in.wait()
+
+    low, high = pl.ds(0, HALF_IN), pl.ds(HALF_IN, HALF_IN)
+
+    def gather(c, i):
+        owner = (x, x, x, x, left, right)[i]
+        part = (low, high, high, low, low, high)[i]
+        target = (right, right, left, left, right, left)[i]
+        ref = inbox.at[c, owner, part]
+        return pltpu.make_async_remote_copy(
+            src_ref=ref,
+            dst_ref=ref,
+            send_sem=asend.at[c, i],
+            recv_sem=arecv.at[c, i],
+            device_id=(me, target),
+            device_id_type=MESH,
+        )
+
+    head, tail = pl.ds(0, HALF_OUT), pl.ds(HALF_OUT, CHUNK_ROWS - HALF_OUT)
+
+    def reduce(c, i):
+        source = (to_far.at[c, head], to_far.at[c, tail], to_right.at[c], to_left.at[c])[i]
+        landing = (far_a.at[c], far_b.at[c], from_left.at[c], from_right.at[c])[i]
+        target = (right, left, right, left)[i]
+        return pltpu.make_async_remote_copy(
+            src_ref=source,
+            dst_ref=landing,
+            send_sem=rsend.at[c, i],
+            recv_sem=rrecv.at[c, i],
+            device_id=(me, target),
+            device_id_type=MESH,
+        )
+
+    def give_back(k):
+        return pltpu.make_async_remote_copy(
+            src_ref=outbox.at[lax.div(k, PER), block(lax.rem(k, PER))],
+            dst_ref=back.at[block(k)],
+            send_sem=bsend.at[k],
+            recv_sem=brecv.at[k],
+            device_id=(behind(k), x),
+            device_id_type=MESH,
+        )
+
+    own_out = pltpu.make_async_copy(
+        outbox.at[0, pl.ds(0, MAIN)], back.at[pl.ds(0, MAIN)], local_sem.at[1]
+    )
+
+    def project(act, quarter):
+        columns = pl.ds(pl.multiple_of(quarter * cols, cols), cols)
+        return jnp.dot(act, down[:, columns], preferred_element_type=jnp.float32)
+
+    def compute(c):
+        tails = jnp.concatenate([inbox[c, m, :, cols:] for m in range(4)], axis=1)
+        tails = jnp.dot(sort[...], tails, preferred_element_type=jnp.float32).astype(jnp.bfloat16)
+        for m in range(4):
+            extra = jnp.concatenate(
+                [
+                    tails[g * CHUNK_OVER : (g + 1) * CHUNK_OVER, m * LANES : (m + 1) * LANES]
+                    for g in range(groups)
+                ],
+                axis=1,
+            )
+            rows = jnp.concatenate([inbox[c, m, :, :cols], extra], axis=0)
+            part = jnp.dot(
+                rows, gate_up[m * cols : (m + 1) * cols, :], preferred_element_type=jnp.float32
+            )
+            if m == 0:
+                acc[...] = part
+            else:
+                acc[...] += part
+        gate, up = acc[:, :ff], acc[:, ff:]
+        act = (gate / (1.0 + jnp.exp(-gate)) * up).astype(jnp.bfloat16)
+        to_far[c] = project(act, far).astype(jnp.bfloat16)
+        reduce(c, 0).start()
+        reduce(c, 1).start()
+        to_right[c] = project(act, right).astype(jnp.bfloat16)
+        to_left[c] = project(act, left).astype(jnp.bfloat16)
+        own[c] = project(act, x)
+
+    @pl.loop(0, CHUNKS + 4)
+    def _(t):
+        @pl.when(t < CHUNKS)
+        def _():
+            @pl.loop(0, PER)
+            def _(j):
+                @pl.when(t * PER + j > 0)
+                def _():
+                    dispatch(t * PER + j).wait_recv()
+
+            for i in (0, 2, 1, 3):
+                gather(t, i).start()
+
+        @pl.when((t >= 1) & (t < CHUNKS + 1))
+        def _():
+            c = t - 1
+            gather(c, 0).wait_recv()
+            gather(c, 4).start()
+            gather(c, 2).wait_recv()
+            gather(c, 5).start()
+
+        @pl.when(t == 2)
+        def _():
+            for copy in weights:
+                copy.wait()
+
+        @pl.when((t >= 2) & (t < CHUNKS + 2))
+        def _():
+            c = t - 2
+            for i in (1, 3, 4, 5):
+                gather(c, i).wait_recv()
+            compute(c)
+
+        @pl.when((t >= 3) & (t < CHUNKS + 3))
+        def _():
+            c = t - 3
+            reduce(c, 0).wait_recv()
+            to_right[c, :HALF_OUT] = (
+                to_right[c, :HALF_OUT].astype(jnp.float32) + far_a[c].astype(jnp.float32)
+            ).astype(jnp.bfloat16)
+            reduce(c, 2).start()
+            reduce(c, 1).wait_recv()
+            to_left[c, HALF_OUT:] = (
+                to_left[c, HALF_OUT:].astype(jnp.float32) + far_b[c].astype(jnp.float32)
+            ).astype(jnp.bfloat16)
+            reduce(c, 3).start()
+
+        @pl.when(t >= 4)
+        def _():
+            c = t - 4
+            reduce(c, 2).wait_recv()
+            reduce(c, 3).wait_recv()
+            total = (
+                own[c] + from_left[c].astype(jnp.float32) + from_right[c].astype(jnp.float32)
+            ).astype(jnp.bfloat16)
+            outbox[c, :, :cols] = total[:CHUNK_MAIN]
+            extra = jnp.concatenate(
+                [total[CHUNK_MAIN:, g * LANES : (g + 1) * LANES] for g in range(groups)], axis=0
+            )
+            outbox[c, :, cols:] = jnp.dot(
+                unsort[...], extra, preferred_element_type=jnp.float32
+            ).astype(jnp.bfloat16)
+
+            @pl.when(c == 0)
+            def _():
+                own_out.start()
+
+            @pl.loop(0, PER)
+            def _(j):
+                @pl.when(c * PER + j > 0)
+                def _():
+                    give_back(c * PER + j).start()
+
+    own_out.wait()
+
+    @pl.loop(1, EXPERTS)
+    def _(k):
+        give_back(k).wait_recv()
+
+    @pl.loop(1, EXPERTS)
+    def _(k):
+        dispatch(k).wait_send()
+        give_back(k).wait_send()
+
+    @pl.loop(0, CHUNKS)
+    def _(c):
+        for i in range(6):
+            gather(c, i).wait_send()
+        for i in range(4):
+            reduce(c, i).wait_send()
+
+
+def experts(packed, w_gate, w_up, w_down):
+    width = packed.shape[1]
+    cols = width - LANES
+    ff, model_width = w_down.shape
+    order = overflow_order()
+    rows = CHUNK_ROWS
+    bf16, f32 = jnp.bfloat16, jnp.float32
+    dma = pltpu.SemaphoreType.DMA
+    anywhere = pl.BlockSpec(memory_space=pl.ANY)
+    onchip = pl.BlockSpec(memory_space=pltpu.VMEM)
+    return pl.pallas_call(
+        expert_kernel,
+        out_shape=jax.ShapeDtypeStruct(packed.shape, bf16),
+        in_specs=[anywhere] * 4 + [onchip] * 2,
+        out_specs=anywhere,
+        scratch_shapes=[
+            pltpu.VMEM((CHUNKS, 4, CHUNK_MAIN, width), bf16),
+            pltpu.VMEM((model_width, 2 * ff), bf16),
+            pltpu.VMEM((ff, model_width), bf16),
+            pltpu.VMEM((rows, 2 * ff), f32),
+            pltpu.VMEM((CHUNKS, rows, cols), bf16),
+            pltpu.VMEM((CHUNKS, rows, cols), bf16),
+            pltpu.VMEM((CHUNKS, rows, cols), bf16),
+            pltpu.VMEM((CHUNKS, rows, cols), f32),
+            pltpu.VMEM((CHUNKS, HALF_OUT, cols), bf16),
+            pltpu.VMEM((CHUNKS, rows - HALF_OUT, cols), bf16),
+            pltpu.VMEM((CHUNKS, rows, cols), bf16),
+            pltpu.VMEM((CHUNKS, rows, cols), bf16),
+            pltpu.VMEM((CHUNKS, CHUNK_MAIN, width), bf16),
+            dma((3,)),
+            dma((2,)),
+            dma((EXPERTS,)),
+            dma((EXPERTS,)),
+            dma((CHUNKS, 6)),
+            dma((CHUNKS, 6)),
+            dma((CHUNKS, 4)),
+            dma((CHUNKS, 4)),
+            dma((EXPERTS,)),
+            dma((EXPERTS,)),
+        ],
+        compiler_params=pltpu.CompilerParams(
+            collective_id=1, has_side_effects=True, vmem_limit_bytes=58 << 20
+        ),
+    )(packed, w_gate, w_up, w_down, jnp.asarray(order, bf16), jnp.asarray(order.T, bf16))
+
+
 def per_device(
     attn_heads, out_proj, residual, norm_gain, route_ids, route_weights, w_gate, w_up, w_down
 ):
     tokens, model_width = residual.shape
     members = lax.axis_size("tensor")
     member = lax.axis_index("tensor")
+    place = lax.axis_index("expert")
     cols = model_width // members
     groups = cols // LANES
     rows = EXPERTS * MAIN
 
-    rank, weight = routing(route_ids, route_weights)
+    relative = ((route_ids // RING - place // RING) % ROWS_Y) * RING + (
+        route_ids % RING - place % RING
+    ) % RING
+    rank, weight = routing(relative, route_weights)
     row = jnp.arange(rows, dtype=jnp.int32)
     slot = row % MAIN
     spread = jnp.repeat(rank, MAIN, axis=1)
@@ -69,28 +375,8 @@
     over = jnp.zeros((rows, LANES), jnp.bfloat16)
     for g in range(groups):
         over = jnp.where(own_group == g, wide[:, g * LANES : (g + 1) * LANES], over)
-    packed = jnp.concatenate([main, over], axis=1).reshape(EXPERTS, MAIN, cols + LANES)
-    arrived = lax.all_to_all(packed, "expert", split_axis=0, concat_axis=0, tiled=True)
-    full = lax.all_gather(arrived.reshape(rows, cols + LANES), "tensor", axis=0)
-    main_in = jnp.concatenate([full[m, :, :cols] for m in range(members)], axis=1)
-    over_in = jnp.transpose(
-        full[:, :, cols:].reshape(members, EXPERTS * OVER, groups, LANES), (1, 0, 2, 3)
-    ).reshape(EXPERTS * OVER, model_width)
-    inputs = jnp.concatenate([main_in, over_in], axis=0)
-    gate = jnp.dot(inputs, w_gate[0], preferred_element_type=jnp.float32)
-    up = jnp.dot(inputs, w_up[0], preferred_element_type=jnp.float32)
-    act = (jax.nn.silu(gate) * up).astype(jnp.bfloat16)
-    down = w_down[0].reshape(-1, members, cols)
-    parts = jnp.stack(
-        [jnp.dot(act, down[:, m], preferred_element_type=jnp.float32) for m in range(members)]
-    ).astype(jnp.bfloat16)
-    summed = lax.psum_scatter(parts, "tensor", scatter_dimension=0, tiled=True)[0]
-    back = jnp.concatenate(
-        [summed[:rows], summed[rows:].reshape(rows, LANES)], axis=1
-    ).reshape(EXPERTS, MAIN, cols + LANES)
-    returned = lax.all_to_all(back, "expert", split_axis=0, concat_axis=0, tiled=True).reshape(
-        rows, cols + LANES
-    )
+    packed = jnp.concatenate([main, over], axis=1)
+    returned = experts(packed, w_gate[0], w_up[0], w_down[0])
     high = row_weight.astype(jnp.bfloat16)
     low = (row_weight - high.astype(jnp.float32)).astype(jnp.bfloat16)
     mixture = 0.0

time: 546 us -> 362 us (0.66)
  waiting for transfers between devices: 336 us -> 105 us
  Pallas kernels: 0 us -> 203 us
  blocking collectives: 77.7 us -> 7.42 us
  matrix products: 62.3 us -> 16.7 us
  local copies, waits for them, and re-layouts: 26.1 us -> 2.47 us
  starting transfers between devices: 11 us -> 0.04 us
  other arithmetic: 18.2 us -> 11.1 us
    pallas_call x0 -> x1, Pallas kernels: none -> 203 us  [experts(): pl.pallas_call(expert_kernel, out_shape=jax.ShapeDtypeStruct(packed.shape...]
    reduce_scatter x1 -> x0, waiting for transfers between devices: 92.7 us -> none  [per_device(): lax.psum_scatter(parts, 'tensor', scatter_dimension=0, tiled=True)[0]]
    all_gather x1 -> x0, waiting for transfers between devices: 84.6 us -> none  [per_device(): full = lax.all_gather(arrived.reshape(rows, cols + LANES), 'tensor', axis=0)]
    all_to_all x1 -> x0, blocking collectives: 71.2 us -> none  [per_device(): lax.all_to_all(packed, 'expert', split_axis=0, concat_axis=0, tiled=True)]
    all_to_all x1 -> x0, waiting for transfers between devices: 51.9 us -> none  [per_device(): lax.all_to_all(back, 'expert', split_axis=0, concat_axis=0, tiled=True)]
    dot_general x6 -> x0, matrix products: 43.1 us -> none  [the longest x1 19.2 us: per_device(): gate = jnp.dot(inputs, w_gate[0], preferred_element_type=jnp.float32)]
    all_to_all x1 -> x0, starting transfers between devices: 10.6 us -> none  [per_device(): lax.all_to_all(back, 'expert', split_axis=0, concat_axis=0, tiled=True)]
  transfers between devices with their start and end apart: 5 -> 2, of which waited for: 5 -> 2; matrix products, arithmetic and copies ran while one was open for 3% -> 2% of each run, Pallas kernels for 0% -> 0%
where the time goes in v2:
time: 362 us; the launch traced here: 360 us
  Pallas kernels  203 us (56%)
  waiting for transfers between devices  105 us (29%)
  matrix products  16.7 us (5%)
  between operations  13.9 us (4%)
  other arithmetic  11.1 us (3%)
  blocking collectives  7.42 us (2%)
    pallas_call x1, Pallas kernels, experts(): pl.pallas_call(expert_kernel, out_shape=jax.ShapeDtypeStruct(packed.shape...  203 us
    all_gather x1, waiting for transfers between devices, per_device(): lax.all_gather(out_proj, 'expert', axis=1, tiled=True)  90.1 us
    reduce_scatter x1, waiting for transfers between devices, per_device(): lax.psum_scatter(jnp.transpose(heads_out.reshape(tokens, members, cols),...  14.4 us
    psum x1, blocking collectives, per_device(): lax.psum(jnp.sum(hidden * hidden, axis=-1, keepdims=True), 'tensor')  7.42 us
  transfers between devices with their start and end apart: 2, of which 2 were waited for; matrix products, arithmetic and copies ran while one was open for 2% of the time, Pallas kernels for 0%

profile of v2, /device:TPU:1, one launch (start us, length us, event | category | flops | bytes accessed | tf_op | source)
XLA Modules:
  0.0 360.1 jit_solution(16716983694126938499)
XLA Ops:
  6.5 0.7 all-gather.2.cloned.1.call-update
  7.3 90.1 %all-gather.2.cloned.1.call-done = bf16[1024,4096]{0,1:T(8,128)(2,1)} async-done(((bf16[1024,64]{0,1:T(8,128)(2,1)}), bf16[1024,4096]{0,1:T(8,128)(2,1)}) %all-gather.2.cloned.1.call-update) | async-done | bytes 8388624 | tf_op jit(solution)/shard_map/all_gather | solution.py:353
  97.5 6.2 %convolution_convert_fusion = bf16[128,4096]{1,0:T(8,128)(2,1)S(1)} fusion(bf16[128,1024]{1,0:T(8,128)(2,1)S(1)} %copy-done, bf16[1024,4096]{0,1:T(8,128)(2,1)} %all-gather.2.cloned.1.call-done), kind=kOutput, calls=%fused_computation | convolution fusion | flops 1074266112 | bytes 9699328 | tf_op jit(solution)/shard_map/dot_general | solution.py:351
  103.7 1.1 copy.94
  104.9 0.7 dynamic_slice.7
  105.8 1.3 bitcast_compare_fusion.1
  107.2 0.5 copy-done.15
  107.8 4.2 %fusion.29 = (bf16[128,1024]{0,1:T(8,128)(2,1)S(1)}, bf16[128,1024]{0,1:T(8,128)(2,1)}, bf16[128,1024]{0,1:T(8,128)(2,1)}, bf16[128,1024]{0,1:T(8,128)(2,1)}, bf...) fusion(f32[128,64]{0,1:T(8,128)S(1)} %get-tuple-element.6, ...), kind=kLoop, calls=%fused_computation.43 | loop fusion | flops 4194304 | bytes 4800512 | tf_op jit(solution)/shard_map/jit(_where)/select_n | solution.py:385
  112.0 14.4 %reduce-scatter.2.cloned.1.call-done = bf16[1,128,1024]{2,1,0:T(8,128)(2,1)} async-done(((bf16[4,128,1024]{2,1,0:T(8,128)(2,1)}), bf16[1,128,1024]{2,1,0:T(8,128)(2,1)}) %reduce-scatter.2.cloned.1.call-update) | async-done | bytes 262160 | tf_op jit(solution)/shard_map/reduce_scatter | solution.py:356
  126.5 1.7 multiply_reduce_fusion
  128.1 7.4 %psum.7 = f32[128,1]{0,1:T(1,128)} all-reduce(f32[128,1]{0,1:T(1,128)} %bitcast.147), channel_id=1, replica_groups=mesh['expert'=64,'tensor'=4] {'tensor'}, use_global_device_ids=true, to_apply=%region_5.6 | all-reduce | flops 128 | bytes 1024 | tf_op jit(solution)/shard_map/psum | solution.py:365
  135.6 0.7 rsqrt_bitcast_fusion
  136.3 1.8 convolution_convert_fusion.1
  138.2 1.5 fusion.54
  139.7 0.8 convolution_convert_fusion.2
  140.4 1.7 pad_maximum_fusion.packed
  142.1 203.1 %shard_map.109 = bf16[1024,1152]{1,0:T(8,128)(2,1)} custom-call(bf16[1024,1152]{1,0:T(8,128)(2,1)} %pad_maximum_fusion.packed, bf16[4096,384]{1,0:T(8,128)(2,1)} %bitcast.144, bf16[4096,384]{1,0:T(8,128)(2,1)} %bitcast.145, bf16[384,4096]{1,0:T(8,128)(2,1)} %bitcast.146, bf16[256,256]{1,0:T(8,128)(2,1)} %constant.193.clone.sort, ...), custom_call_target="tpu_custom_call" | custom-call | tf_op jit(solution)/shard_map/pallas_call | solution.py:293
  345.3 2.2 fusion
  348.4 0.3 convolution_dynamic-update-slice_fusion.13
  348.7 0.3 convolution_dynamic-update-slice_fusion.12
  349.3 0.3 convolution_dynamic-update-slice_fusion.10
  349.8 0.3 convolution_dynamic-update-slice_fusion.8
  350.9 0.3 convolution_dynamic-update-slice_fusion.3
  352.0 1.2 fusion.16
  (75 shorter events, 3.5 us)
Async XLA Ops:
  6.5 90.9 %copy-start = (bf16[128,1024]{1,0:T(8,128)(2,1)S(1)}, bf16[128,1024]{1,0:T(8,128)(2,1)}, u32[]{:S(2)}) copy-start(bf16[128,1024]{1,0:T(8,128)(2,1)} %param.11) | copy-start | bytes 786436
  6.5 90.9 %all-gather.2.cloned.1.call-start = ((), (), s32[]{:S(2)}) async-start(), calls=%async_computation.1 | async-start | bytes 8519680 | tf_op jit(solution)/shard_map/all_gather | solution.py:353
  7.3 119.2 %reduce-scatter.2.cloned.1.call-start = ((), (), s32[]{:S(2)}) async-start(), calls=%async_computation.2 | async-start | bytes 1310720 | tf_op jit(solution)/shard_map/reduce_scatter | solution.py:356
  103.7 1.2 copy-start.14
  103.7 1.9 copy-start.25
  107.2 0.6 copy-start.23
  107.8 18.7 %copy-start.3 = (bf16[128,4096]{1,0:T(8,128)(2,1)S(1)}, bf16[128,4096]{1,0:T(8,128)(2,1)}, u32[]{:S(2)}) copy-start(bf16[128,4096]{1,0:T(8,128)(2,1)} %param.13) | copy-start | bytes 3145732
  135.6 2.5 copy-start.16
  135.6 2.5 copy-start.18
  135.6 2.6 copy-start.20
  135.6 2.6 copy-start.22
  135.6 2.6 copy-start.24
  136.3 3.4 copy-start.2
  142.1 203.1 %copy-start.13 = (bf16[128,1024]{0,1:T(8,128)(2,1)S(1)}, bf16[128,1024]{0,1:T(8,128)(2,1)}, u32[]{:S(2)}) copy-start(bf16[128,1024]{0,1:T(8,128)(2,1)} %get-tuple-element.24) | copy-start | bytes 786436
  142.1 205.4 %copy-start.12 = (bf16[128,1024]{0,1:T(8,128)(2,1)S(1)}, bf16[128,1024]{0,1:T(8,128)(2,1)}, u32[]{:S(2)}) copy-start(bf16[128,1024]{0,1:T(8,128)(2,1)} %get-tuple-element.39) | copy-start | bytes 786436
  345.2 2.3 copy-start.1
  345.2 2.6 copy-start.11
  345.2 2.9 copy-start.10
  345.2 3.2 copy-start.9
  345.3 3.4 copy-start.8
  345.3 3.7 %copy-start.7 = (bf16[128,1024]{0,1:T(8,128)(2,1)S(1)}, bf16[128,1024]{0,1:T(8,128)(2,1)}, u32[]{:S(2)}) copy-start(bf16[128,1024]{0,1:T(8,128)(2,1)} %get-tuple-element.47) | copy-start | bytes 786436
  347.5 1.8 copy-start.6
  347.5 2.0 copy-start.5
  347.5 2.3 copy-start.4
  (4 other events, 2.3 us)
Sparse Core Ops, SparseCore 0:
  10.1 87.2 all-gather.1
  105.0 21.4 reduce-scatter.1

commit v3 on v2

--- a/solution.py
+++ b/solution.py
@@ -45,6 +45,269 @@
             for c in range(OVER):
                 matrix[g * CHUNK_OVER + s * OVER + c, s * MAIN + c * groups + g] = 1.0
     return matrix
+
+
+def attention_kernel(
+    heads_hbm, proj_hbm, residual_hbm, gain_hbm, hidden_out, normed_out,
+    shard, sibling_shard, weight, heads, to_far, to_right, to_left, own,
+    far_a, far_b, from_left, from_right, mine, arrived, residual, gain, squares,
+    local_sem, shard_sem, zsend, zrecv, csend, crecv, hsend, hrecv, rsend, rrecv, wsem, nsend, nrecv,
+):
+    me = lax.axis_index("expert")
+    x = lax.axis_index("tensor")
+    y, zc = lax.div(me, RING), lax.rem(me, RING)
+    core, z = lax.rem(zc, 2), lax.div(zc, 2)
+    depth = RING // 2
+    right, left, far = lax.rem(x + 1, 4), lax.rem(x + 3, 4), lax.rem(x + 2, 4)
+    sibling = me + 1 - 2 * core
+    cols = weight.shape[1]
+    half = weight.shape[0] // 2
+    tokens = heads.shape[1]
+
+    def along_z(step):
+        return y * RING + lax.rem(z + depth + step, depth) * 2 + core
+
+    def along_y(step):
+        return lax.rem(y + step, ROWS_Y) * RING + zc
+
+    partner = (x * RING + zc, y)
+    local = [
+        pltpu.make_async_copy(proj_hbm, shard, local_sem.at[0]),
+        pltpu.make_async_copy(heads_hbm, heads.at[y], local_sem.at[1]),
+        pltpu.make_async_copy(
+            residual_hbm.at[:, pl.ds(pl.multiple_of(x * cols, cols), cols)], residual, local_sem.at[2]
+        ),
+        pltpu.make_async_copy(
+            gain_hbm.at[:, pl.ds(pl.multiple_of(x * cols, cols), cols)], gain, local_sem.at[3]
+        ),
+    ]
+    for copy in local:
+        copy.start()
+
+    barrier = pltpu.get_barrier_semaphore()
+    for device in (sibling, along_z(1), along_z(-1), along_y(1), along_y(2), along_y(3)):
+        pl.semaphore_signal(barrier, inc=1, device_id=(device, x), device_id_type=MESH)
+    for m in (right, left, far):
+        pl.semaphore_signal(barrier, inc=1, device_id=(me, m), device_id_type=MESH)
+
+    @pl.when(x != y)
+    def _():
+        pl.semaphore_signal(barrier, inc=1, device_id=partner, device_id_type=MESH)
+        pl.semaphore_wait(barrier, 10)
+
+    @pl.when(x == y)
+    def _():
+        pl.semaphore_wait(barrier, 9)
+
+    def remote(source, landing, send, recv, device):
+        return pltpu.make_async_remote_copy(
+            src_ref=source,
+            dst_ref=landing,
+            send_sem=send,
+            recv_sem=recv,
+            device_id=device,
+            device_id_type=MESH,
+        )
+
+    swap_shard = remote(
+        shard.at[pl.ds(pl.multiple_of((1 - core) * half, half), half)],
+        sibling_shard,
+        shard_sem.at[0],
+        shard_sem.at[1],
+        (sibling, x),
+    )
+    local[0].wait()
+    swap_shard.start()
+    local[1].wait()
+
+    def share_heads(i):
+        return remote(heads.at[y], heads.at[y], hsend.at[i], hrecv.at[i], (along_y(i + 1), x))
+
+    for i in (1, 0, 2):
+        share_heads(i).start()
+
+    def piece(owner, part):
+        start = core * half + (half // 2 if part == 2 else 0)
+        count = half if part == 0 else half // 2
+        return weight.at[
+            pl.ds(pl.multiple_of(start, half // 2), count),
+            pl.ds(pl.multiple_of(owner * LANES, LANES), LANES),
+        ]
+
+    def ring(direction, s):
+        offset = -(s - 1) if direction == 0 else s - 1
+        ref = piece(
+            lax.rem(z + depth + offset, depth), (1 + direction) if s == depth // 2 else 0
+        )
+        target = along_z(1 if direction == 0 else -1)
+        return remote(ref, ref, zsend.at[direction, s - 1], zrecv.at[direction, s - 1], (target, x))
+
+    def across(direction, s):
+        offset = -s if direction == 0 else s
+        ref = piece(
+            lax.rem(z + depth + offset, depth), (1 + direction) if s == depth // 2 else 0
+        )
+        i = 5 * direction + s
+        return remote(ref, ref, csend.at[i], crecv.at[i], (sibling, x))
+
+    width = shard.shape[1]
+    row = lax.broadcasted_iota(jnp.int32, (width, LANES), 0)
+    lane = lax.broadcasted_iota(jnp.int32, (width, LANES), 1)
+    put_own = (lane == row + width * core).astype(jnp.bfloat16)
+    put_other = (lane == row + width * (1 - core)).astype(jnp.bfloat16)
+    swap_shard.wait_recv()
+    both = jnp.dot(
+        shard[pl.ds(pl.multiple_of(core * half, half), half), :],
+        put_own,
+        preferred_element_type=jnp.float32,
+    ) + jnp.dot(sibling_shard[...], put_other, preferred_element_type=jnp.float32)
+    weight[
+        pl.ds(pl.multiple_of(core * half, half), half),
+        pl.ds(pl.multiple_of(z * LANES, LANES), LANES),
+    ] = both.astype(jnp.bfloat16)
+    ring(0, 1).start()
+    ring(1, 1).start()
+    across(0, 0).start()
+    for s in range(1, depth // 2 + 1):
+        for direction in (0, 1):
+            ring(direction, s).wait_recv()
+            if s < depth // 2:
+                ring(direction, s + 1).start()
+            across(direction, s).start()
+    handed = [(0, 0)] + [(d, s) for s in range(1, depth // 2 + 1) for d in (0, 1)]
+    for i in (0, 2, 1):
+        share_heads(i).wait_recv()
+    for d, s in handed:
+        across(d, s).wait_recv()
+
+    def partial(block):
+        return jnp.dot(heads[block], weight[...], preferred_element_type=jnp.float32)
+
+    part = tokens // 2
+
+    def reduce(i):
+        source = (to_far.at[pl.ds(0, part)], to_far.at[pl.ds(part, part)], to_right, to_left)[i]
+        landing = (far_a, far_b, from_left, from_right)[i]
+        target = (right, left, right, left)[i]
+        return remote(source, landing, rsend.at[i], rrecv.at[i], (me, target))
+
+    to_far[...] = partial(far).astype(jnp.bfloat16)
+    reduce(0).start()
+    reduce(1).start()
+    via_right = partial(right)
+    reduce(0).wait_recv()
+    to_right[:part] = (via_right[:part] + far_a[...].astype(jnp.float32)).astype(jnp.bfloat16)
+    to_right[part:] = via_right[part:].astype(jnp.bfloat16)
+    reduce(2).start()
+    via_left = partial(left)
+    reduce(1).wait_recv()
+    to_left[:part] = via_left[:part].astype(jnp.bfloat16)
+    to_left[part:] = (via_left[part:] + far_b[...].astype(jnp.float32)).astype(jnp.bfloat16)
+    reduce(3).start()
+    own[...] = partial(x)
+    reduce(2).wait_recv()
+    reduce(3).wait_recv()
+    mine[...] = (
+        own[...] + from_left[...].astype(jnp.float32) + from_right[...].astype(jnp.float32)
+    ).astype(jnp.bfloat16)
+    exchange = remote(mine, arrived, wsem.at[0], wsem.at[1], partner)
+
+    @pl.when(x != y)
+    def _():
+        exchange.start()
+        exchange.wait_recv()
+        exchange.wait_send()
+
+    @pl.when(x == y)
+    def _():
+        arrived[...] = mine[...]
+
+    local[2].wait()
+    local[3].wait()
+    hidden = residual[...].astype(jnp.float32) + arrived[...].astype(jnp.float32)
+    hidden_out[...] = hidden
+    squares[0] = jnp.broadcast_to(
+        jnp.sum(hidden * hidden, axis=-1, keepdims=True), (tokens, LANES)
+    )
+
+    def share_squares(i):
+        return remote(
+            squares.at[0], squares.at[i + 1], nsend.at[i], nrecv.at[i], (me, (right, far, left)[i])
+        )
+
+    for i in range(3):
+        share_squares(i).start()
+    for i in range(3):
+        share_squares(i).wait_recv()
+    mean = (squares[0] + squares[1] + squares[2] + squares[3]) / (4 * cols)
+    scale = lax.rsqrt(mean + 1e-06)[:, :1]
+    normed_out[...] = (hidden * scale * gain[...]).astype(jnp.bfloat16)
+
+    swap_shard.wait_send()
+    for i in range(3):
+        share_heads(i).wait_send()
+        share_squares(i).wait_send()
+    for d, s in handed:
+        across(d, s).wait_send()
+    for s in range(1, depth // 2 + 1):
+        for direction in (0, 1):
+            ring(direction, s).wait_send()
+    for i in range(4):
+        reduce(i).wait_send()
+
+
+def attention(attn_heads, out_proj, residual, norm_gain):
+    tokens, depth = attn_heads.shape
+    cols = residual.shape[1] // 4
+    bf16, f32 = jnp.bfloat16, jnp.float32
+    dma = pltpu.SemaphoreType.DMA
+    anywhere = pl.BlockSpec(memory_space=pl.ANY)
+    onchip = pl.BlockSpec(memory_space=pltpu.VMEM)
+    block = pltpu.VMEM((tokens, cols), bf16)
+    return pl.pallas_call(
+        attention_kernel,
+        out_shape=(
+            jax.ShapeDtypeStruct((tokens, cols), f32),
+            jax.ShapeDtypeStruct((tokens, cols), bf16),
+        ),
+        in_specs=[anywhere] * 4,
+        out_specs=(onchip, onchip),
+        scratch_shapes=[
+            pltpu.VMEM(out_proj.shape, bf16),
+            pltpu.VMEM((depth // 2, out_proj.shape[1]), bf16),
+            pltpu.VMEM((depth, cols), bf16),
+            pltpu.VMEM((ROWS_Y, tokens, depth), bf16),
+            block,
+            block,
+            block,
+            pltpu.VMEM((tokens, cols), f32),
+            pltpu.VMEM((tokens // 2, cols), bf16),
+            pltpu.VMEM((tokens // 2, cols), bf16),
+            block,
+            block,
+            block,
+            block,
+            block,
+            pltpu.VMEM((1, cols), f32),
+            pltpu.VMEM((4, tokens, LANES), f32),
+            dma((4,)),
+            dma((2,)),
+            dma((2, 4)),
+            dma((2, 4)),
+            dma((10,)),
+            dma((10,)),
+            dma((3,)),
+            dma((3,)),
+            dma((4,)),
+            dma((4,)),
+            dma((2,)),
+            dma((3,)),
+            dma((3,)),
+        ],
+        compiler_params=pltpu.CompilerParams(
+            collective_id=2, has_side_effects=True, vmem_limit_bytes=32 << 20
+        ),
+    )(attn_heads, out_proj, residual, norm_gain[None, :])
 
 
 def expert_kernel(
@@ -331,7 +594,6 @@
 ):
     tokens, model_width = residual.shape
     members = lax.axis_size("tensor")
-    member = lax.axis_index("tensor")
     place = lax.axis_index("expert")
     cols = model_width // members
     groups = cols // LANES
@@ -348,22 +610,7 @@
     over_hit = spread == (MAIN + slot // groups)[None, :]
     row_weight = jnp.repeat(weight, MAIN, axis=1)
 
-    heads_out = jnp.dot(
-        attn_heads,
-        lax.all_gather(out_proj, "expert", axis=1, tiled=True),
-        preferred_element_type=jnp.float32,
-    ).astype(jnp.bfloat16)
-    attn_out = lax.psum_scatter(
-        jnp.transpose(heads_out.reshape(tokens, members, cols), (1, 0, 2)),
-        "tensor",
-        scatter_dimension=0,
-        tiled=True,
-    )[0].astype(jnp.float32)
-    own_residual = lax.dynamic_slice_in_dim(residual, member * cols, cols, 1)
-    own_gain = lax.dynamic_slice_in_dim(norm_gain, member * cols, cols, 0)
-    hidden = own_residual.astype(jnp.float32) + attn_out
-    squares = lax.psum(jnp.sum(hidden * hidden, axis=-1, keepdims=True), "tensor")
-    normed = (hidden * lax.rsqrt(squares / model_width + 1e-06) * own_gain).astype(jnp.bfloat16)
+    hidden, normed = attention(attn_heads, out_proj, residual, norm_gain)
 
     main = jnp.einsum(
         "tr,td->rd", main_hit.astype(jnp.bfloat16), normed, preferred_element_type=jnp.float32

time: 362 us -> 281 us (0.78)
  waiting for transfers between devices: 105 us -> 0 us
  Pallas kernels: 203 us -> 261 us
  between operations: 13.9 us -> 0.26 us
  matrix products: 16.7 us -> 7.64 us
  blocking collectives: 7.42 us -> 0 us
    all_gather x1 -> x0, waiting for transfers between devices: 90.1 us -> none  [per_device(): lax.all_gather(out_proj, 'expert', axis=1, tiled=True)]
    pallas_call x0 -> x1, Pallas kernels: none -> 60.4 us  [attention(): pl.pallas_call(attention_kernel, out_shape=(jax.ShapeDtypeStruct((tokens,...]
    reduce_scatter x1 -> x0, waiting for transfers between devices: 14.4 us -> none  [per_device(): lax.psum_scatter(jnp.transpose(heads_out.reshape(tokens, members, cols),...]
    psum x1 -> x0, blocking collectives: 7.42 us -> none  [per_device(): lax.psum(jnp.sum(hidden * hidden, axis=-1, keepdims=True), 'tensor')]
    dot_general x1 -> x0, matrix products: 6.23 us -> none  [per_device(): jnp.dot(attn_heads, lax.all_gather(out_proj, 'expert', axis=1, tiled=True...]
  transfers between devices with their start and end apart: 2 -> 0, of which waited for: 2 -> 0; matrix products, arithmetic and copies ran while one was open for 2% -> 0% of each run, Pallas kernels for 0% -> 0%
where the time goes in v3:
time: 281 us; the launch traced here: 280 us
  Pallas kernels  261 us (93%)
  other arithmetic  8.08 us (3%)
  matrix products  7.64 us (3%)
  local copies, waits for them, and re-layouts  3.97 us (1%)
    pallas_call x1, Pallas kernels, experts(): pl.pallas_call(expert_kernel, out_shape=jax.ShapeDtypeStruct(packed.shape...  200 us
    pallas_call x1, Pallas kernels, attention(): pl.pallas_call(attention_kernel, out_shape=(jax.ShapeDtypeStruct((tokens,...  60.4 us

profile of v3, /device:TPU:1, one launch (start us, length us, event | category | flops | bytes accessed | tf_op | source)
XLA Modules:
  0.0 280.5 jit_solution(12436759103854797446)
XLA Ops:
  0.0 0.7 fusion.59
  0.7 0.7 reduce_sum.28
  1.4 0.7 broadcast_divide_fusion
  2.3 0.7 bitcast_compare_fusion.1
  3.0 1.1 copy.55.proj_hbm
  4.1 1.2 copy-done
  5.3 0.9 copy-done.1
  6.3 0.7 copy-done.2
  7.0 60.4 %shard_map.109 = (f32[128,1024]{1,0:T(8,128)S(1)}, bf16[128,1024]{1,0:T(8,128)(2,1)S(1)}) custom-call(bf16[128,1024]{1,0:T(8,128)(2,1)S(1)} %copy-done.1, bf16[1024,64]{1,0:T(8,128)(2,1)S(1)} %copy.55.proj_hbm, bf16[128,4096]{1,0:T(8,128)(2,1)S(1)} %copy-done, f32[1,4096]{1,0:T(1,128)S(1)} %bitcast.126), custom_call_target="tpu_custom_call" | custom-call | tf_op jit(solution)/shard_map/pallas_call | solution.py:267
  67.4 0.7 convolution_convert_fusion
  68.2 1.5 fusion.54
  69.7 0.7 convolution_convert_fusion.1
  70.4 1.6 pad_maximum_fusion.packed
  72.0 200.1 %shard_map.110 = bf16[1024,1152]{1,0:T(8,128)(2,1)} custom-call(bf16[1024,1152]{1,0:T(8,128)(2,1)} %pad_maximum_fusion.packed, bf16[4096,384]{1,0:T(8,128)(2,1)} %bitcast.127, bf16[4096,384]{1,0:T(8,128)(2,1)} %bitcast.128, bf16[384,4096]{1,0:T(8,128)(2,1)} %bitcast.129, bf16[256,256]{1,0:T(8,128)(2,1)} %constant.180.clone.sort, ...), custom_call_target="tpu_custom_call" | custom-call | tf_op jit(solution)/shard_map/pallas_call | solution.py:556
  272.1 2.1 fusion.29
  274.2 0.3 convolution_dynamic-update-slice_fusion.15
  274.5 0.3 convolution_dynamic-update-slice_fusion.14
  275.4 0.3 convolution_dynamic-update-slice_fusion.11
  276.2 0.3 convolution_dynamic-update-slice_fusion.8
  276.5 0.3 convolution_dynamic-update-slice_fusion.7
  276.8 0.3 convolution_dynamic-update-slice_fusion.6
  277.6 0.3 convolution_dynamic-update-slice_fusion.3
  278.8 0.5 fusion
  279.2 1.2 fusion.16
  (21 shorter events, 2.7 us)
Async XLA Ops:
  4.1 1.2 copy-start
  5.3 0.9 copy-start.1
  6.3 0.7 copy-start.2
  272.1 2.1 copy-start.3

commit v4 on v3

v4 whole, which is shorter than its diff:
```python
import jax
import jax.numpy as jnp
import numpy as np
from jax import lax
from jax.experimental import pallas as pl
from jax.experimental.pallas import tpu as pltpu
from jax.sharding import PartitionSpec as P

MESH = pl.DeviceIdType.MESH
EXPERTS = 64
RING = 16
ROWS_Y = EXPERTS // RING
MAIN = 16
OVER = 2
LANES = 128
GROUPS = 8
SPLIT = 768
DEPTH = 8
PER = 8
CHUNK_MAIN = PER * MAIN
CHUNK_OVER = PER * OVER
CHUNK_ROWS = CHUNK_MAIN + CHUNK_OVER
HALF_IN = CHUNK_MAIN // 2
HALF_OUT = CHUNK_ROWS // 2 // 16 * 16


def routing(ids, route_weights):
    count = ids.shape[0]
    hits = (ids[:, :, None] == jnp.arange(EXPERTS, dtype=jnp.int32)[None, None, :]).astype(
        jnp.float32
    )
    chosen = jnp.sum(hits, axis=1)
    weights = route_weights / jnp.sum(route_weights, axis=-1, keepdims=True)
    weight = jnp.sum(hits * weights[:, :, None], axis=1)
    order = jnp.arange(count, dtype=jnp.int32)
    earlier = (order[None, :] < order[:, None]).astype(jnp.bfloat16)
    rank = jnp.dot(earlier, chosen.astype(jnp.bfloat16), preferred_element_type=jnp.float32)
    rank = jnp.where(chosen > 0, rank, -1.0)
    return rank.astype(jnp.int32), weight


def overflow_order():
    groups = GROUPS
    matrix = np.zeros((CHUNK_MAIN, CHUNK_MAIN), np.float32)
    for g in range(groups):
        for s in range(PER):
            for c in range(OVER):
                matrix[g * CHUNK_OVER + s * OVER + c, s * MAIN + c * groups + g] = 1.0
    return matrix


def attention_kernel(
    heads_hbm, proj_hbm, residual_hbm, gain_hbm, hidden_out, normed_out,
    shard, sibling_shard, weight, heads, to_far, to_right, to_left, own,
    far_a, far_b, from_left, from_right, mine, arrived, residual, gain, squares,
    shared, shared_residual, shared_gain,
    local_sem, shard_sem, zsend, zrecv, csend, crecv, hsend, hrecv, rsend, rrecv, wsem, nsend, nrecv,
    ssend, srecv,
):
    me = lax.axis_index("expert")
    x = lax.axis_index("tensor")
    y, zc = lax.div(me, RING), lax.rem(me, RING)
    core, z = lax.rem(zc, 2), lax.div(zc, 2)
    depth = RING // 2
    right, left, far = lax.rem(x + 1, 4), lax.rem(x + 3, 4), lax.rem(x + 2, 4)
    sibling = me + 1 - 2 * core
    cols = weight.shape[1]
    half = weight.shape[0] // 2
    tokens = heads.shape[1]

    def along_z(step):
        return y * RING + lax.rem(z + depth + step, depth) * 2 + core

    def along_y(step):
        return lax.rem(y + step, ROWS_Y) * RING + zc

    partner = (x * RING + zc, y)
    local = [
        pltpu.make_async_copy(proj_hbm, shard, local_sem.at[0]),
        pltpu.make_async_copy(heads_hbm, heads.at[y], local_sem.at[1]),
        pltpu.make_async_copy(
            residual_hbm.at[:, pl.ds(pl.multiple_of(x * cols, cols), cols)], residual, local_sem.at[2]
        ),
        pltpu.make_async_copy(
            gain_hbm.at[:, pl.ds(pl.multiple_of(x * cols, cols), cols)], gain, local_sem.at[3]
        ),
    ]
    share = cols - SPLIT
    for m in range(4):
        local.append(
            pltpu.make_async_copy(
                residual_hbm.at[:, pl.ds(m * cols + SPLIT, share)],
                shared_residual.at[:, pl.ds(m * share, share)],
                local_sem.at[4 + m],
            )
        )
        local.append(
            pltpu.make_async_copy(
                gain_hbm.at[:, pl.ds(m * cols + SPLIT, share)],
                shared_gain.at[:, pl.ds(m * share, share)],
                local_sem.at[8 + m],
            )
        )
    for copy in local:
        copy.start()

    barrier = pltpu.get_barrier_semaphore()
    for device in (sibling, along_z(1), along_z(-1), along_y(1), along_y(2), along_y(3)):
        pl.semaphore_signal(barrier, inc=1, device_id=(device, x), device_id_type=MESH)
    for m in (right, left, far):
        pl.semaphore_signal(barrier, inc=1, device_id=(me, m), device_id_type=MESH)

    @pl.when(x != y)
    def _():
        pl.semaphore_signal(barrier, inc=1, device_id=partner, device_id_type=MESH)
        pl.semaphore_wait(barrier, 10)

    @pl.when(x == y)
    def _():
        pl.semaphore_wait(barrier, 9)

    def remote(source, landing, send, recv, device):
        return pltpu.make_async_remote_copy(
            src_ref=source,
            dst_ref=landing,
            send_sem=send,
            recv_sem=recv,
            device_id=device,
            device_id_type=MESH,
        )

    swap_shard = remote(
        shard.at[pl.ds(pl.multiple_of((1 - core) * half, half), half)],
        sibling_shard,
        shard_sem.at[0],
        shard_sem.at[1],
        (sibling, x),
    )
    local[0].wait()
    swap_shard.start()
    local[1].wait()

    def share_heads(i):
        return remote(heads.at[y], heads.at[y], hsend.at[i], hrecv.at[i], (along_y(i + 1), x))

    for i in (1, 0, 2):
        share_heads(i).start()

    def piece(owner, part):
        start = core * half + (half // 2 if part == 2 else 0)
        count = half if part == 0 else half // 2
        return weight.at[
            pl.ds(pl.multiple_of(start, half // 2), count),
            pl.ds(pl.multiple_of(owner * LANES, LANES), LANES),
        ]

    def ring(direction, s):
        offset = -(s - 1) if direction == 0 else s - 1
        ref = piece(
            lax.rem(z + depth + offset, depth), (1 + direction) if s == depth // 2 else 0
        )
        target = along_z(1 if direction == 0 else -1)
        return remote(ref, ref, zsend.at[direction, s - 1], zrecv.at[direction, s - 1], (target, x))

    def across(direction, s):
        offset = -s if direction == 0 else s
        ref = piece(
            lax.rem(z + depth + offset, depth), (1 + direction) if s == depth // 2 else 0
        )
        i = 5 * direction + s
        return remote(ref, ref, csend.at[i], crecv.at[i], (sibling, x))

    width = shard.shape[1]
    row = lax.broadcasted_iota(jnp.int32, (width, LANES), 0)
    lane = lax.broadcasted_iota(jnp.int32, (width, LANES), 1)
    put_own = (lane == row + width * core).astype(jnp.bfloat16)
    put_other = (lane == row + width * (1 - core)).astype(jnp.bfloat16)
    swap_shard.wait_recv()
    both = jnp.dot(
        shard[pl.ds(pl.multiple_of(core * half, half), half), :],
        put_own,
        preferred_element_type=jnp.float32,
    ) + jnp.dot(sibling_shard[...], put_other, preferred_element_type=jnp.float32)
    weight[
        pl.ds(pl.multiple_of(core * half, half), half),
        pl.ds(pl.multiple_of(z * LANES, LANES), LANES),
    ] = both.astype(jnp.bfloat16)
    ring(0, 1).start()
    ring(1, 1).start()
    across(0, 0).start()
    for s in range(1, depth // 2 + 1):
        for direction in (0, 1):
            ring(direction, s).wait_recv()
            if s < depth // 2:
                ring(direction, s + 1).start()
            across(direction, s).start()
    handed = [(0, 0)] + [(d, s) for s in range(1, depth // 2 + 1) for d in (0, 1)]
    for i in (0, 2, 1):
        share_heads(i).wait_recv()
    for d, s in handed:
        across(d, s).wait_recv()

    def partial(block):
        return jnp.dot(heads[block], weight[...], preferred_element_type=jnp.float32)

    part = tokens // 2

    def reduce(i):
        source = (to_far.at[pl.ds(0, part)], to_far.at[pl.ds(part, part)], to_right, to_left)[i]
        landing = (far_a, far_b, from_left, from_right)[i]
        target = (right, left, right, left)[i]
        return remote(source, landing, rsend.at[i], rrecv.at[i], (me, target))

    to_far[...] = partial(far).astype(jnp.bfloat16)
    reduce(0).start()
    reduce(1).start()
    via_right = partial(right)
    reduce(0).wait_recv()
    to_right[:part] = (via_right[:part] + far_a[...].astype(jnp.float32)).astype(jnp.bfloat16)
    to_right[part:] = via_right[part:].astype(jnp.bfloat16)
    reduce(2).start()
    via_left = partial(left)
    reduce(1).wait_recv()
    to_left[:part] = via_left[:part].astype(jnp.bfloat16)
    to_left[part:] = (via_left[part:] + far_b[...].astype(jnp.float32)).astype(jnp.bfloat16)
    reduce(3).start()
    own[...] = partial(x)
    reduce(2).wait_recv()
    reduce(3).wait_recv()
    mine[...] = (
        own[...] + from_left[...].astype(jnp.float32) + from_right[...].astype(jnp.float32)
    ).astype(jnp.bfloat16)
    exchange = remote(mine, arrived, wsem.at[0], wsem.at[1], partner)

    @pl.when(x != y)
    def _():
        exchange.start()
        exchange.wait_recv()
        exchange.wait_send()

    @pl.when(x == y)
    def _():
        arrived[...] = mine[...]

    shared[x] = arrived[:, SPLIT:]

    def share_features(i):
        return remote(
            shared.at[x], shared.at[x], ssend.at[i], srecv.at[i], (me, (right, far, left)[i])
        )

    for i in range(3):
        share_features(i).start()
    for copy in local[2:]:
        copy.wait()
    hidden = residual[...].astype(jnp.float32) + arrived[...].astype(jnp.float32)
    hidden_out[...] = hidden
    squares[0] = jnp.broadcast_to(
        jnp.sum(hidden * hidden, axis=-1, keepdims=True), (tokens, LANES)
    )

    def share_squares(i):
        return remote(
            squares.at[0], squares.at[i + 1], nsend.at[i], nrecv.at[i], (me, (right, far, left)[i])
        )

    for i in range(3):
        share_squares(i).start()
    for i in range(3):
        share_squares(i).wait_recv()
        share_features(i).wait_recv()
    mean = (squares[0] + squares[1] + squares[2] + squares[3]) / (4 * cols)
    scale = lax.rsqrt(mean + 1e-06)[:, :1]
    normed_out[:, :SPLIT] = (hidden[:, :SPLIT] * scale * gain[:, :SPLIT]).astype(jnp.bfloat16)
    for m in range(4):
        lanes = slice(m * share, (m + 1) * share)
        value = shared_residual[:, lanes].astype(jnp.float32) + shared[m].astype(jnp.float32)
        normed_out[:, SPLIT + m * share : SPLIT + (m + 1) * share] = (
            value * scale * shared_gain[:, lanes]
        ).astype(jnp.bfloat16)

    swap_shard.wait_send()
    for i in range(3):
        share_heads(i).wait_send()
        share_squares(i).wait_send()
        share_features(i).wait_send()
    for d, s in handed:
        across(d, s).wait_send()
    for s in range(1, depth // 2 + 1):
        for direction in (0, 1):
            ring(direction, s).wait_send()
    for i in range(4):
        reduce(i).wait_send()


def attention(attn_heads, out_proj, residual, norm_gain):
    tokens, depth = attn_heads.shape
    cols = residual.shape[1] // 4
    bf16, f32 = jnp.bfloat16, jnp.float32
    dma = pltpu.SemaphoreType.DMA
    anywhere = pl.BlockSpec(memory_space=pl.ANY)
    onchip = pl.BlockSpec(memory_space=pltpu.VMEM)
    block = pltpu.VMEM((tokens, cols), bf16)
    return pl.pallas_call(
        attention_kernel,
        out_shape=(
            jax.ShapeDtypeStruct((tokens, cols), f32),
            jax.ShapeDtypeStruct((tokens, SPLIT + 4 * (cols - SPLIT)), bf16),
        ),
        in_specs=[anywhere] * 4,
        out_specs=(onchip, onchip),
        scratch_shapes=[
            pltpu.VMEM(out_proj.shape, bf16),
            pltpu.VMEM((depth // 2, out_proj.shape[1]), bf16),
            pltpu.VMEM((depth, cols), bf16),
            pltpu.VMEM((ROWS_Y, tokens, depth), bf16),
            block,
            block,
            block,
            pltpu.VMEM((tokens, cols), f32),
            pltpu.VMEM((tokens // 2, cols), bf16),
            pltpu.VMEM((tokens // 2, cols), bf16),
            block,
            block,
            block,
            block,
            block,
            pltpu.VMEM((1, cols), f32),
            pltpu.VMEM((4, tokens, LANES), f32),
            pltpu.VMEM((4, tokens, cols - SPLIT), bf16),
            pltpu.VMEM((tokens, 4 * (cols - SPLIT)), bf16),
            pltpu.VMEM((1, 4 * (cols - SPLIT)), f32),
            dma((12,)),
            dma((2,)),
            dma((2, 4)),
            dma((2, 4)),
            dma((10,)),
            dma((10,)),
            dma((3,)),
            dma((3,)),
            dma((4,)),
            dma((4,)),
            dma((2,)),
            dma((3,)),
            dma((3,)),
            dma((3,)),
            dma((3,)),
        ],
        compiler_params=pltpu.CompilerParams(
            collective_id=2, has_side_effects=True, vmem_limit_bytes=32 << 20
        ),
    )(attn_heads, out_proj, residual, norm_gain[None, :])


def expert_kernel(
    normed, routes_in, hidden, gate_hbm, up_hbm, down_hbm, sort, unsort, out,
    tokens_in, routes, packed, inbox, inner, gate_up, down, acc,
    to_far, to_right, to_left, own, far_a, far_b, from_left, from_right,
    returned, planes, total, staged, quarters,
    local_sem, zsend, zrecv, tsend, trecv, ysend, yrecv, asend, arecv,
    rsend, rrecv, bsend, brecv, msend, mrecv, fsend, frecv,
):
    me = lax.axis_index("expert")
    x = lax.axis_index("tensor")
    y, zc = lax.div(me, RING), lax.rem(me, RING)
    core, z = lax.rem(zc, 2), lax.div(zc, 2)
    right, left, far = lax.rem(x + 1, 4), lax.rem(x + 3, 4), lax.rem(x + 2, 4)
    ff = gate_hbm.shape[1]
    cols = hidden.shape[1]
    share = cols - SPLIT
    inner_width = SPLIT + LANES
    first = inner_width
    last = first + 4 * share
    bf16, f32 = jnp.bfloat16, jnp.float32

    def along_z(step):
        return y * RING + lax.rem(z + DEPTH + step, DEPTH) * 2 + core

    def distance(i):
        odd = lax.rem(i, 2)
        return lax.rem(odd * lax.div(i + 1, 2) + (1 - odd) * (DEPTH - lax.div(i, 2)), DEPTH)

    def plane(dy, dc):
        return lax.rem(y + ROWS_Y + dy, ROWS_Y) * RING + z * 2 + lax.rem(core + dc, 2)

    def remote(source, landing, send, recv, device):
        return pltpu.make_async_remote_copy(
            src_ref=source,
            dst_ref=landing,
            send_sem=send,
            recv_sem=recv,
            device_id=device,
            device_id_type=MESH,
        )

    weights = [
        pltpu.make_async_copy(gate_hbm, gate_up.at[:, pl.ds(0, ff)], local_sem.at[0]),
        pltpu.make_async_copy(up_hbm, gate_up.at[:, pl.ds(ff, ff)], local_sem.at[1]),
        pltpu.make_async_copy(down_hbm, down, local_sem.at[2]),
    ]
    load_tokens = pltpu.make_async_copy(normed, tokens_in.at[0], local_sem.at[3])
    load_routes = pltpu.make_async_copy(routes_in.at[0], routes.at[0], local_sem.at[4])
    load_tokens.start()
    load_routes.start()
    for copy in weights:
        copy.start()

    barrier = pltpu.get_barrier_semaphore()

    @pl.loop(1, DEPTH)
    def _(i):
        pl.semaphore_signal(barrier, inc=1, device_id=(along_z(i), x), device_id_type=MESH)
        pl.semaphore_signal(
            barrier,
            inc=1,
            device_id=(plane(lax.div(i, 2), lax.rem(i, 2)), x),
            device_id_type=MESH,
        )

    for m in (right, far, left):
        pl.semaphore_signal(barrier, inc=1, device_id=(me, m), device_id_type=MESH)
    pl.semaphore_wait(barrier, 2 * (DEPTH - 1) + 3)

    def block(k):
        return pl.ds(pl.multiple_of(k * MAIN, MAIN), MAIN)

    def send_routes(i):
        return remote(
            routes_in.at[i], routes.at[i], tsend.at[i], trecv.at[i], (along_z(distance(i)), x)
        )

    def ring(i, before=None):
        before = lax.rem(i + DEPTH - 2, DEPTH) if before is None else before
        return remote(
            tokens_in.at[before],
            tokens_in.at[i],
            zsend.at[i],
            zrecv.at[i],
            (along_z(2 * lax.rem(i, 2) - 1), x),
        )

    middle = tokens_in.shape[1] // 2

    def ring_far(side):
        rows = pl.ds(side * middle, middle)
        return remote(
            tokens_in.at[DEPTH - 3 + side, rows],
            tokens_in.at[DEPTH - 1, rows],
            zsend.at[DEPTH - 1 + side],
            zrecv.at[DEPTH - 1 + side],
            (along_z(1 - 2 * side), x),
        )

    load_tokens.wait()
    ring(1, 0).start()
    ring(2, 0).start()

    @pl.loop(1, DEPTH)
    def _(i):
        send_routes(i).start()

    load_routes.wait()

    def exchange(i, k):
        return remote(
            packed.at[i, block(k)],
            inbox.at[i, block(k)],
            ysend.at[i, k],
            yrecv.at[i, k],
            (plane(lax.div(k, 2), lax.rem(k, 2)), x),
        )

    def give_back(i, k):
        return remote(
            packed.at[i, block(k)],
            returned.at[i, block(k)],
            bsend.at[i, k],
            brecv.at[i, k],
            (plane(-lax.div(k, 2), lax.rem(k, 2)), x),
        )

    low, high = pl.ds(0, HALF_IN), pl.ds(HALF_IN, HALF_IN)

    def gather(c, i):
        owner = (x, x, x, x, left, right)[i]
        part = (low, high, high, low, low, high)[i]
        target = (right, right, left, left, right, left)[i]
        ref = inner.at[c, owner, part]
        return remote(ref, ref, asend.at[c, i], arecv.at[c, i], (me, target))

    head, tail = pl.ds(0, HALF_OUT), pl.ds(HALF_OUT, CHUNK_ROWS - HALF_OUT)

    def reduce(c, i):
        source = (to_far.at[c, head], to_far.at[c, tail], to_right.at[c], to_left.at[c])[i]
        landing = (far_a.at[c], far_b.at[c], from_left.at[c], from_right.at[c])[i]
        return remote(
            source, landing, rsend.at[c, i], rrecv.at[c, i], (me, (right, left, right, left)[i])
        )

    def send_plane(i):
        return remote(
            tokens_in.at[i], planes.at[i], msend.at[i], mrecv.at[i], (along_z(-distance(i)), x)
        )

    def send_quarter(i):
        m = (right, far, left)[i]
        return remote(
            staged.at[:, pl.ds(pl.multiple_of(m * share, share), share)],
            quarters.at[i],
            fsend.at[i],
            frecv.at[i],
            (me, m),
        )

    square = (CHUNK_MAIN, CHUNK_MAIN)
    row = lax.broadcasted_iota(jnp.int32, square, 0)
    row_slot = (row & (MAIN - 1)).astype(f32)
    row_over = (MAIN + ((row & (MAIN - 1)) >> 3)).astype(f32)
    row_group = row & (GROUPS - 1)
    lane_group = lax.broadcasted_iota(jnp.int32, square, 1) & (GROUPS - 1)

    def spread(values):
        return jnp.broadcast_to(values[:, None, :], (PER, MAIN, LANES)).reshape(square)

    def dot(a, b):
        return jnp.dot(a, b, preferred_element_type=f32)

    def pick(i):
        rank = spread(routes[i, :PER])
        tokens = tokens_in[i]
        chosen = dot(jnp.where(rank == row_slot, 1.0, 0.0).astype(bf16), tokens)
        packed[i, :, :SPLIT] = chosen[:, :SPLIT].astype(bf16)
        packed[i, :, first:last] = chosen[:, SPLIT:].astype(bf16)
        wide = dot(jnp.where(rank == row_over, 1.0, 0.0).astype(bf16), tokens)
        for start, count, lane in ((0, SPLIT // LANES, SPLIT), (SPLIT, GROUPS, last)):
            tile = jnp.zeros(square, f32)
            for g in range(count):
                piece = wide[:, start + g * LANES : start + (g + 1) * LANES]
                tile = jnp.where(row_group == g, piece, tile)
            packed[i, :, lane : lane + LANES] = tile.astype(bf16)
        inbox[i, :MAIN] = packed[i, :MAIN]

        @pl.loop(1, PER)
        def _(k):
            exchange(i, k).start()

    def project(act, quarter):
        columns = pl.ds(pl.multiple_of(quarter * cols, cols), cols)
        return dot(act, down[:, columns])

    def compute(c):
        @pl.loop(1, PER)
        def _(k):
            exchange(c, k).wait_send()

        tails = jnp.concatenate(
            [inner[c, m, :, SPLIT:] for m in range(4)] + [inbox[c, :, last:]], axis=1
        )
        tails = dot(sort[...], tails).astype(bf16)

        def tail_piece(g, tile):
            return tails[g * CHUNK_OVER : (g + 1) * CHUNK_OVER, tile * LANES : (tile + 1) * LANES]

        per_share = share // LANES
        for m in range(4):
            extra = [tail_piece(g, m) for g in range(SPLIT // LANES)] + [
                tail_piece(m * per_share + g, 4) for g in range(per_share)
            ]
            body = jnp.concatenate(
                [
                    inner[c, m, :, :SPLIT],
                    inbox[c, :, first + m * share : first + (m + 1) * share],
                ],
                axis=1,
            )
            rows = jnp.concatenate([body, jnp.concatenate(extra, axis=1)], axis=0)
            part = dot(rows, gate_up[m * cols : (m + 1) * cols, :])
            if m == 0:
                acc[...] = part
            else:
                acc[...] += part
        gate, up = acc[:, :ff], acc[:, ff:]
        act = (gate / (1.0 + jnp.exp(-gate)) * up).astype(bf16)

        def keep_share(quarter, value):
            lanes = pl.ds(pl.multiple_of(first + quarter * share, LANES), share)
            packed[c, :, lanes] = value[:CHUNK_MAIN, SPLIT:].astype(bf16)
            staging = pl.ds(pl.multiple_of(quarter * share, share), share)
            staged[:CHUNK_OVER, staging] = value[CHUNK_MAIN:, SPLIT:].astype(bf16)

        value = project(act, far)
        to_far[c] = value[:, :SPLIT].astype(bf16)
        reduce(c, 0).start()
        reduce(c, 1).start()
        keep_share(far, value)
        value = project(act, right)
        to_right[c] = value[:, :SPLIT].astype(bf16)
        keep_share(right, value)
        value = project(act, left)
        to_left[c] = value[:, :SPLIT].astype(bf16)
        keep_share(left, value)
        value = project(act, x)
        own[c] = value[:, :SPLIT]
        keep_share(x, value)
        over = staged[:CHUNK_OVER, :]
        over = jnp.concatenate(
            [over[:, g * LANES : (g + 1) * LANES] for g in range(GROUPS)], axis=0
        )
        packed[c, :, last:] = dot(unsort[...], over).astype(bf16)

    def finish(c):
        reduce(c, 2).wait_recv()
        reduce(c, 3).wait_recv()
        value = (
            own[c] + from_left[c].astype(f32) + from_right[c].astype(f32)
        ).astype(bf16)
        packed[c, :, :SPLIT] = value[:CHUNK_MAIN]
        count = SPLIT // LANES
        over = jnp.concatenate(
            [value[CHUNK_MAIN:, g * LANES : (g + 1) * LANES] for g in range(count)]
            + [jnp.zeros(((GROUPS - count) * CHUNK_OVER, LANES), bf16)],
            axis=0,
        )
        packed[c, :, SPLIT:first] = dot(unsort[...], over).astype(bf16)
        returned[c, :MAIN] = packed[c, :MAIN]

        @pl.loop(1, PER)
        def _(k):
            give_back(c, k).start()

    def combine(c):
        @pl.loop(1, PER)
        def _(k):
            give_back(c, k).wait_recv()

        rank, weight = spread(routes[c, :PER]), spread(routes[c, PER:])
        rows = returned[c]
        whole = jnp.where(rank == row_slot, weight, 0.0).T
        over = jnp.where(rank == row_over, weight, 0.0).T
        high_part = whole.astype(bf16)
        low_part = (whole - high_part.astype(f32)).astype(bf16)
        mixed = dot(high_part, rows) + dot(low_part, rows)
        tiles = jnp.concatenate([rows[:, SPLIT:first], rows[:, last:]], axis=1)
        extra = []
        for g in range(GROUPS):
            picked = jnp.where(lane_group == g, over, 0.0)
            high_part = picked.astype(bf16)
            low_part = (picked - high_part.astype(f32)).astype(bf16)
            extra.append(dot(high_part, tiles) + dot(low_part, tiles))
        count = SPLIT // LANES
        inner_sum = mixed[:, :SPLIT] + jnp.concatenate(
            [extra[g][:, :LANES] for g in range(count)], axis=1
        )
        share_sum = mixed[:, first:last] + jnp.concatenate(
            [extra[g][:, LANES:] for g in range(GROUPS)], axis=1
        )

        @pl.when(c == 0)
        def _():
            total[:, :SPLIT] = inner_sum
            total[:, SPLIT:] = share_sum

        @pl.when((c >= 1) & (c <= DEPTH - 4))
        def _():
            ring(c + 2).wait_send()

        for side in (0, 1):

            @pl.when(c == DEPTH - 3 + side)
            def _():
                ring_far(side).wait_send()

        @pl.when(c > 0)
        def _():
            tokens_in[c, :, :SPLIT] = inner_sum.astype(bf16)
            tokens_in[c, :, SPLIT:] = share_sum.astype(bf16)
            send_plane(c).start()

    pick(0)

    @pl.loop(0, DEPTH + 5)
    def _(t):
        @pl.when(t < DEPTH)
        def _():
            @pl.loop(1, PER)
            def _(k):
                exchange(t, k).wait_recv()

            inner[t, x] = inbox[t, :, :inner_width]
            for i in (0, 2, 1, 3):
                gather(t, i).start()

        @pl.when((t >= 1) & (t < DEPTH + 1))
        def _():
            c = t - 1
            gather(c, 0).wait_recv()
            gather(c, 4).start()
            gather(c, 2).wait_recv()
            gather(c, 5).start()

        @pl.when(t + 1 < DEPTH)
        def _():
            i = t + 1

            @pl.when(i < DEPTH - 1)
            def _():
                ring(i).wait_recv()

            @pl.when(i + 2 < DEPTH - 1)
            def _():
                ring(i + 2).start()

            for side in (0, 1):

                @pl.when(i == DEPTH - 3 + side)
                def _():
                    ring_far(side).start()

                @pl.when(i == DEPTH - 1)
                def _():
                    ring_far(side).wait_recv()

            send_routes(i).wait_recv()
            pick(i)

        @pl.when(t == 2)
        def _():
            for copy in weights:
                copy.wait()

        @pl.when((t >= 2) & (t < DEPTH + 2))
        def _():
            c = t - 2
            for i in (1, 3, 4, 5):
                gather(c, i).wait_recv()
            compute(c)

        @pl.when((t >= 3) & (t < DEPTH + 3))
        def _():
            c = t - 3
            reduce(c, 0).wait_recv()
            to_right[c, :HALF_OUT] = (
                to_right[c, :HALF_OUT].astype(f32) + far_a[c].astype(f32)
            ).astype(bf16)
            reduce(c, 2).start()
            reduce(c, 1).wait_recv()
            to_left[c, HALF_OUT:] = (
                to_left[c, HALF_OUT:].astype(f32) + far_b[c].astype(f32)
            ).astype(bf16)
            reduce(c, 3).start()

        @pl.when((t >= 4) & (t < DEPTH + 4))
        def _():
            finish(t - 4)

        @pl.when(t >= 5)
        def _():
            combine(t - 5)

    @pl.loop(1, DEPTH)
    def _(i):
        send_plane(i).wait_recv()
        total[...] += planes[i].astype(f32)

    staged[...] = total[:, SPLIT:].astype(bf16)
    for i in range(3):
        send_quarter(i).start()
    out[:, :SPLIT] = (hidden[:, :SPLIT] + total[:, :SPLIT]).astype(bf16)
    mixture = total[:, pl.ds(pl.multiple_of(SPLIT + x * share, share), share)]
    for i in range(3):
        send_quarter(i).wait_recv()
        mixture += quarters[i].astype(f32)
    out[:, SPLIT:] = (hidden[:, SPLIT:] + mixture).astype(bf16)

    for i in (1, 2):
        ring(i, 0).wait_send()
    for i in range(3):
        send_quarter(i).wait_send()

    @pl.loop(1, DEPTH)
    def _(i):
        send_routes(i).wait_send()
        send_plane(i).wait_send()

    @pl.loop(0, DEPTH)
    def _(c):
        for i in range(6):
            gather(c, i).wait_send()
        for i in range(4):
            reduce(c, i).wait_send()

        @pl.loop(1, PER)
        def _(k):
            give_back(c, k).wait_send()


def experts(normed, routes, hidden, w_gate, w_up, w_down):
    tokens, wide = normed.shape
    cols = hidden.shape[1]
    ff, model_width = w_down.shape
    order = overflow_order()
    rows = CHUNK_ROWS
    width = wide + 2 * LANES
    bf16, f32 = jnp.bfloat16, jnp.float32
    dma = pltpu.SemaphoreType.DMA
    anywhere = pl.BlockSpec(memory_space=pl.ANY)
    onchip = pl.BlockSpec(memory_space=pltpu.VMEM)
    moved = pltpu.VMEM((DEPTH, rows, SPLIT), bf16)
    return pl.pallas_call(
        expert_kernel,
        out_shape=jax.ShapeDtypeStruct((tokens, cols), bf16),
        in_specs=[anywhere] * 2 + [onchip] + [anywhere] * 3 + [onchip] * 2,
        out_specs=onchip,
        scratch_shapes=[
            pltpu.VMEM((DEPTH, tokens, wide), bf16),
            pltpu.VMEM((DEPTH, 2 * PER, LANES), f32),
            pltpu.VMEM((DEPTH, CHUNK_MAIN, width), bf16),
            pltpu.VMEM((DEPTH, CHUNK_MAIN, width), bf16),
            pltpu.VMEM((DEPTH, 4, CHUNK_MAIN, SPLIT + LANES), bf16),
            pltpu.VMEM((model_width, 2 * ff), bf16),
            pltpu.VMEM((ff, model_width), bf16),
            pltpu.VMEM((rows, 2 * ff), f32),
            moved,
            moved,
            moved,
            pltpu.VMEM((DEPTH, rows, SPLIT), f32),
            pltpu.VMEM((DEPTH, HALF_OUT, SPLIT), bf16),
            pltpu.VMEM((DEPTH, rows - HALF_OUT, SPLIT), bf16),
            moved,
            moved,
            pltpu.VMEM((DEPTH, CHUNK_MAIN, width), bf16),
            pltpu.VMEM((DEPTH, tokens, wide), bf16),
            pltpu.VMEM((tokens, wide), f32),
            pltpu.VMEM((tokens, wide - SPLIT), bf16),
            pltpu.VMEM((3, tokens, cols - SPLIT), bf16),
            dma((5,)),
            dma((DEPTH + 1,)),
            dma((DEPTH + 1,)),
            dma((DEPTH,)),
            dma((DEPTH,)),
            dma((DEPTH, PER)),
            dma((DEPTH, PER)),
            dma((DEPTH, 6)),
            dma((DEPTH, 6)),
            dma((DEPTH, 4)),
            dma((DEPTH, 4)),
            dma((DEPTH, PER)),
            dma((DEPTH, PER)),
            dma((DEPTH,)),
            dma((DEPTH,)),
            dma((3,)),
            dma((3,)),
        ],
        compiler_params=pltpu.CompilerParams(
            collective_id=1, has_side_effects=True, vmem_limit_bytes=60 << 20
        ),
    )(normed, routes, hidden, w_gate, w_up, w_down, jnp.asarray(order, bf16), jnp.asarray(order.T, bf16))


def per_device(
    attn_heads, out_proj, residual, norm_gain, route_ids, route_weights, w_gate, w_up, w_down
):
    place = lax.axis_index("expert")
    ahead_z = (route_ids % RING // 2 - place % RING // 2) % DEPTH
    chunk = jnp.where(
        ahead_z == 0, 0, jnp.where(ahead_z <= DEPTH // 2, 2 * ahead_z - 1, 2 * (DEPTH - ahead_z))
    )
    ahead_y = (route_ids // RING - place // RING) % ROWS_Y
    relative = chunk * PER + ahead_y * 2 + (route_ids - place) % 2
    rank, weight = routing(relative, route_weights)
    routes = jnp.concatenate(
        [
            rank.T.astype(jnp.float32).reshape(DEPTH, PER, -1),
            weight.T.reshape(DEPTH, PER, -1),
        ],
        axis=1,
    )
    hidden, normed = attention(attn_heads, out_proj, residual, norm_gain)
    return experts(normed, routes, hidden, w_gate[0], w_up[0], w_down[0])


def solution(mesh):
    placed = (
        P("expert", "tensor"),
        P("tensor", "expert"),
        P("expert", None),
        P(),
        P("expert", None),
        P("expert", None),
        P("expert", None, "tensor"),
        P("expert", None, "tensor"),
        P("expert", "tensor", None),
    )
    return jax.shard_map(
        per_device, mesh=mesh, in_specs=placed, out_specs=P("expert", "tensor"), check_vma=False
    )
```

time: 281 us -> 287 us (1.021)
  Pallas kernels: 261 us -> 276 us
  matrix products: 7.64 us -> 0.14 us
  other arithmetic: 8.08 us -> 2.81 us
  local copies, waits for them, and re-layouts: 3.97 us -> 7.18 us
    pallas_call x1, Pallas kernels: 200 us -> 212 us  [experts(): pl.pallas_call(expert_kernel, out_shape=jax.ShapeDtypeStruct((tokens, col...]
    dot_general x20 -> x0, matrix products: 7.49 us -> none  [the longest x16 4.39 us: per_device(): jnp.dot(jnp.where(over_hit & (row % groups == g)[None, :], part, zero), r...]
    pallas_call x1, Pallas kernels: 60.4 us -> 64.3 us  [attention(): pl.pallas_call(attention_kernel, out_shape=(jax.ShapeDtypeStruct((tokens,...]
    select_n x3 -> x0, other arithmetic: 3.59 us -> none  [the longest x1 2.09 us: per_device(): pick = jnp.where(main_hit, part, zero)]
    unnamed x9 -> x12, local copies, waits for them, and re-layouts: 3.97 us -> 7.18 us
where the time goes in v4:
time: 287 us
  Pallas kernels  276 us (96%)
  local copies, waits for them, and re-layouts  7.18 us (3%)
    pallas_call x1, Pallas kernels, experts(): pl.pallas_call(expert_kernel, out_shape=jax.ShapeDtypeStruct((tokens, col...  212 us
    pallas_call x1, Pallas kernels, attention(): pl.pallas_call(attention_kernel, out_shape=(jax.ShapeDtypeStruct((tokens,...  64.3 us
    unnamed x12, local copies, waits for them, and re-layouts  7.18 us

profile of v4, /device:TPU:1, one launch (start us, length us, event | category | flops | bytes accessed | tf_op | source)
XLA Modules:
  0.0 286.5 jit_solution(11618336638451638772)
XLA Ops:
  0.0 1.1 copy.15.proj_hbm
  1.1 0.0 copy-start
  1.1 1.2 copy-done
  2.3 0.0 copy-start.3
  2.3 0.9 copy-done.3
  3.3 0.0 copy-start.4
  3.3 0.7 copy-done.4
  4.0 64.3 %shard_map.109 = (f32[128,1024]{1,0:T(8,128)S(1)}, bf16[128,1792]{1,0:T(8,128)(2,1)S(1)}) custom-call(bf16[128,1024]{1,0:T(8,128)(2,1)S(1)} %copy-done.3, bf16[1024,64]{1,0:T(8,128)(2,1)S(1)} %copy.15.proj_hbm, bf16[128,4096]{1,0:T(8,128)(2,1)S(1)} %copy-done, f32[1,4096]{1,0:T(1,128)S(1)} %bitcast.11), custom_call_target="tpu_custom_call" | custom-call | tf_op jit(solution)/shard_map/pallas_call | solution.py:304
  68.3 0.0 copy-start.1
  68.3 0.8 copy-done.1
  69.1 0.0 copy-start.2
  69.1 0.8 copy-done.2
  69.8 0.7 fusion.11
  70.6 0.7 reduce_sum.28
  71.3 0.7 broadcast_divide_fusion
  72.0 0.1 fusion.2
  72.2 0.7 pad_maximum_fusion.routes_in
  72.8 212.0 %shard_map.110 = bf16[128,1024]{1,0:T(8,128)(2,1)} custom-call(bf16[128,1792]{1,0:T(8,128)(2,1)} %copy-done.2, f32[8,16,128]{2,1,0:T(8,128)} %pad_maximum_fusion.routes_in, f32[128,1024]{1,0:T(8,128)} %copy-done.1, bf16[4096,384]{1,0:T(8,128)(2,1)} %bitcast.12, bf16[4096,384]{1,0:T(8,128)(2,1)} %bitcast.13, bf16[384,4096]{1,0:T(8,128)(2,1)} %bitcast.14, ...), custom_call_target="tpu_custom_call" | custom-call | tf_op jit(solution)/shard_map/pallas_call | solution.py:809
  284.8 1.7 copy.17
  (1 shorter events, 0.0 us)
Async XLA Ops:
  1.1 1.2 copy-start
  2.3 0.9 copy-start.3
  3.3 0.7 copy-start.4
  68.3 0.8 copy-start.1
  69.1 0.8 copy-start.2

commit v5 on v4

--- a/solution.py
+++ b/solution.py
@@ -1,6 +1,5 @@
 import jax
 import jax.numpy as jnp
-import numpy as np
 from jax import lax
 from jax.experimental import pallas as pl
 from jax.experimental.pallas import tpu as pltpu
@@ -24,33 +23,9 @@
 HALF_OUT = CHUNK_ROWS // 2 // 16 * 16
 
 
-def routing(ids, route_weights):
-    count = ids.shape[0]
-    hits = (ids[:, :, None] == jnp.arange(EXPERTS, dtype=jnp.int32)[None, None, :]).astype(
-        jnp.float32
-    )
-    chosen = jnp.sum(hits, axis=1)
-    weights = route_weights / jnp.sum(route_weights, axis=-1, keepdims=True)
-    weight = jnp.sum(hits * weights[:, :, None], axis=1)
-    order = jnp.arange(count, dtype=jnp.int32)
-    earlier = (order[None, :] < order[:, None]).astype(jnp.bfloat16)
-    rank = jnp.dot(earlier, chosen.astype(jnp.bfloat16), preferred_element_type=jnp.float32)
-    rank = jnp.where(chosen > 0, rank, -1.0)
-    return rank.astype(jnp.int32), weight
-
-
-def overflow_order():
-    groups = GROUPS
-    matrix = np.zeros((CHUNK_MAIN, CHUNK_MAIN), np.float32)
-    for g in range(groups):
-        for s in range(PER):
-            for c in range(OVER):
-                matrix[g * CHUNK_OVER + s * OVER + c, s * MAIN + c * groups + g] = 1.0
-    return matrix
-
-
 def attention_kernel(
-    heads_hbm, proj_hbm, residual_hbm, gain_hbm, hidden_out, normed_out,
+    heads_hbm, proj_hbm, residual_hbm, gain_hbm, route_ids, route_weights,
+    hidden_out, normed_out, routes_out,
     shard, sibling_shard, weight, heads, to_far, to_right, to_left, own,
     far_a, far_b, from_left, from_right, mine, arrived, residual, gain, squares,
     shared, shared_residual, shared_gain,
@@ -64,8 +39,8 @@
     depth = RING // 2
     right, left, far = lax.rem(x + 1, 4), lax.rem(x + 3, 4), lax.rem(x + 2, 4)
     sibling = me + 1 - 2 * core
-    cols = weight.shape[1]
-    half = weight.shape[0] // 2
+    cols = from_left.shape[1]
+    half = weight.shape[1] // 2
     tokens = heads.shape[1]
 
     def along_z(step):
@@ -149,10 +124,7 @@
     def piece(owner, part):
         start = core * half + (half // 2 if part == 2 else 0)
         count = half if part == 0 else half // 2
-        return weight.at[
-            pl.ds(pl.multiple_of(start, half // 2), count),
-            pl.ds(pl.multiple_of(owner * LANES, LANES), LANES),
-        ]
+        return weight.at[owner, pl.ds(pl.multiple_of(start, half // 2), count)]
 
     def ring(direction, s):
         offset = -(s - 1) if direction == 0 else s - 1
@@ -181,13 +153,38 @@
         put_own,
         preferred_element_type=jnp.float32,
     ) + jnp.dot(sibling_shard[...], put_other, preferred_element_type=jnp.float32)
-    weight[
-        pl.ds(pl.multiple_of(core * half, half), half),
-        pl.ds(pl.multiple_of(z * LANES, LANES), LANES),
-    ] = both.astype(jnp.bfloat16)
+    weight[z, pl.ds(pl.multiple_of(core * half, half), half)] = both.astype(jnp.bfloat16)
     ring(0, 1).start()
     ring(1, 1).start()
     across(0, 0).start()
+    square = (tokens, LANES)
+    lane = lax.broadcasted_iota(jnp.int32, square, 1)
+    earlier = jnp.where(lane < lax.broadcasted_iota(jnp.int32, square, 0), 1.0, 0.0)
+    ids = route_ids[...]
+    ahead_z = (((ids & (RING - 1)) >> 1) + depth - z) & (depth - 1)
+    chunk = jnp.where(
+        ahead_z == 0, 0, jnp.where(ahead_z <= depth // 2, 2 * ahead_z - 1, 2 * (depth - ahead_z))
+    )
+    ahead_y = ((ids >> 4) + ROWS_Y - y) & (ROWS_Y - 1)
+    relative = chunk * PER + ahead_y * 2 + ((ids + 2 - core) & 1)
+    shares = route_weights[...] / jnp.sum(route_weights[...], axis=-1, keepdims=True)
+    chosen = jnp.zeros(square, jnp.float32)
+    scaled = jnp.zeros(square, jnp.float32)
+    for k in range(ids.shape[1]):
+        hit = lane == relative[:, k : k + 1]
+        chosen = jnp.where(hit, 1.0, chosen)
+        scaled = jnp.where(hit, shares[:, k : k + 1], scaled)
+    rank = jnp.dot(
+        earlier.astype(jnp.bfloat16),
+        chosen.astype(jnp.bfloat16),
+        preferred_element_type=jnp.float32,
+    )
+    rank = jnp.where(chosen > 0, rank, -1.0).T
+    scaled = scaled.T
+    for i in range(depth):
+        routes_out[i, :PER] = rank[i * PER : (i + 1) * PER]
+        routes_out[i, PER:] = scaled[i * PER : (i + 1) * PER]
+
     for s in range(1, depth // 2 + 1):
         for direction in (0, 1):
             ring(direction, s).wait_recv()
@@ -201,7 +198,17 @@
         across(d, s).wait_recv()
 
     def partial(block):
-        return jnp.dot(heads[block], weight[...], preferred_element_type=jnp.float32)
+        return jnp.concatenate(
+            [
+                jnp.dot(
+                    heads[block],
+                    jnp.concatenate([weight[i], weight[i + 1]], axis=1),
+                    preferred_element_type=jnp.float32,
+                )
+                for i in range(0, RING // 2, 2)
+            ],
+            axis=1,
+        )
 
     part = tokens // 2
 
@@ -236,7 +243,6 @@
     def _():
         exchange.start()
         exchange.wait_recv()
-        exchange.wait_send()
 
     @pl.when(x == y)
     def _():
@@ -256,8 +262,8 @@
     hidden = residual[...].astype(jnp.float32) + arrived[...].astype(jnp.float32)
     hidden_out[...] = hidden
     squares[0] = jnp.broadcast_to(
-        jnp.sum(hidden * hidden, axis=-1, keepdims=True), (tokens, LANES)
-    )
+        jnp.sum(hidden * hidden, axis=-1, keepdims=True), square
+    ).T[:PER]
 
     def share_squares(i):
         return remote(
@@ -270,7 +276,7 @@
         share_squares(i).wait_recv()
         share_features(i).wait_recv()
     mean = (squares[0] + squares[1] + squares[2] + squares[3]) / (4 * cols)
-    scale = lax.rsqrt(mean + 1e-06)[:, :1]
+    scale = jnp.broadcast_to(lax.rsqrt(mean + 1e-06)[:1], square).T[:, :1]
     normed_out[:, :SPLIT] = (hidden[:, :SPLIT] * scale * gain[:, :SPLIT]).astype(jnp.bfloat16)
     for m in range(4):
         lanes = slice(m * share, (m + 1) * share)
@@ -278,6 +284,10 @@
         normed_out[:, SPLIT + m * share : SPLIT + (m + 1) * share] = (
             value * scale * shared_gain[:, lanes]
         ).astype(jnp.bfloat16)
+
+    @pl.when(x != y)
+    def _():
+        exchange.wait_send()
 
     swap_shard.wait_send()
     for i in range(3):
@@ -293,7 +303,7 @@
         reduce(i).wait_send()
 
 
-def attention(attn_heads, out_proj, residual, norm_gain):
+def attention(attn_heads, out_proj, residual, norm_gain, route_ids, route_weights):
     tokens, depth = attn_heads.shape
     cols = residual.shape[1] // 4
     bf16, f32 = jnp.bfloat16, jnp.float32
@@ -306,13 +316,14 @@
         out_shape=(
             jax.ShapeDtypeStruct((tokens, cols), f32),
             jax.ShapeDtypeStruct((tokens, SPLIT + 4 * (cols - SPLIT)), bf16),
+            jax.ShapeDtypeStruct((DEPTH, 2 * PER, tokens), f32),
         ),
-        in_specs=[anywhere] * 4,
-        out_specs=(onchip, onchip),
+        in_specs=[anywhere] * 4 + [onchip] * 2,
+        out_specs=(onchip, onchip, onchip),
         scratch_shapes=[
             pltpu.VMEM(out_proj.shape, bf16),
             pltpu.VMEM((depth // 2, out_proj.shape[1]), bf16),
-            pltpu.VMEM((depth, cols), bf16),
+            pltpu.VMEM((RING // 2, depth, LANES), bf16),
             pltpu.VMEM((ROWS_Y, tokens, depth), bf16),
             block,
             block,
@@ -326,7 +337,7 @@
             block,
             block,
             pltpu.VMEM((1, cols), f32),
-            pltpu.VMEM((4, tokens, LANES), f32),
+            pltpu.VMEM((4, PER, LANES), f32),
             pltpu.VMEM((4, tokens, cols - SPLIT), bf16),
             pltpu.VMEM((tokens, 4 * (cols - SPLIT)), bf16),
             pltpu.VMEM((1, 4 * (cols - SPLIT)), f32),
@@ -347,16 +358,16 @@
             dma((3,)),
         ],
         compiler_params=pltpu.CompilerParams(
-            collective_id=2, has_side_effects=True, vmem_limit_bytes=32 << 20
+            collective_id=2, has_side_effects=True, vmem_limit_bytes=60 << 20
         ),
-    )(attn_heads, out_proj, residual, norm_gain[None, :])
+    )(attn_heads, out_proj, residual, norm_gain[None, :], route_ids, route_weights)
 
 
 def expert_kernel(
-    normed, routes_in, hidden, gate_hbm, up_hbm, down_hbm, sort, unsort, out,
+    normed, routes_in, hidden, gate_hbm, up_hbm, down_hbm, out,
     tokens_in, routes, packed, inbox, inner, gate_up, down, acc,
     to_far, to_right, to_left, own, far_a, far_b, from_left, from_right,
-    returned, planes, total, staged, quarters,
+    returned, planes, total, summed, staged, quarters,
     local_sem, zsend, zrecv, tsend, trecv, ysend, yrecv, asend, arecv,
     rsend, rrecv, bsend, brecv, msend, mrecv, fsend, frecv,
 ):
@@ -497,10 +508,16 @@
             source, landing, rsend.at[c, i], rrecv.at[c, i], (me, (right, left, right, left)[i])
         )
 
+    half_tokens = tokens_in.shape[1] // 2
+
     def send_plane(i):
-        return remote(
-            tokens_in.at[i], planes.at[i], msend.at[i], mrecv.at[i], (along_z(-distance(i)), x)
-        )
+        slot = (0, 1, 2, 3, 0, 7, 4, 5, 6)[i]
+        step = (0, -1, 1, -2, 2, -3, 1, -1, 1)[i]
+        source, landing = tokens_in.at[min(i, 7)], planes.at[slot]
+        if i >= 7:
+            rows = pl.ds((i - 7) * half_tokens, half_tokens)
+            source, landing = tokens_in.at[7, rows], planes.at[slot, rows]
+        return remote(source, landing, msend.at[i], mrecv.at[i], (along_z(step), x))
 
     def send_quarter(i):
         m = (right, far, left)[i]
@@ -518,6 +535,14 @@
     row_over = (MAIN + ((row & (MAIN - 1)) >> 3)).astype(f32)
     row_group = row & (GROUPS - 1)
     lane_group = lax.broadcasted_iota(jnp.int32, square, 1) & (GROUPS - 1)
+
+    lane = lax.broadcasted_iota(jnp.int32, square, 1)
+
+    def unsorted_row(r):
+        return ((r >> 1) & (PER - 1)) * MAIN + (r & 1) * GROUPS + (r >> 4)
+
+    sort = jnp.where(lane == unsorted_row(row), 1.0, 0.0).astype(bf16)
+    unsort = jnp.where(row == unsorted_row(lane), 1.0, 0.0).astype(bf16)
 
     def spread(values):
         return jnp.broadcast_to(values[:, None, :], (PER, MAIN, LANES)).reshape(square)
@@ -556,7 +581,7 @@
         tails = jnp.concatenate(
             [inner[c, m, :, SPLIT:] for m in range(4)] + [inbox[c, :, last:]], axis=1
         )
-        tails = dot(sort[...], tails).astype(bf16)
+        tails = dot(sort, tails).astype(bf16)
 
         def tail_piece(g, tile):
             return tails[g * CHUNK_OVER : (g + 1) * CHUNK_OVER, tile * LANES : (tile + 1) * LANES]
@@ -606,7 +631,7 @@
         over = jnp.concatenate(
             [over[:, g * LANES : (g + 1) * LANES] for g in range(GROUPS)], axis=0
         )
-        packed[c, :, last:] = dot(unsort[...], over).astype(bf16)
+        packed[c, :, last:] = dot(unsort, over).astype(bf16)
 
     def finish(c):
         reduce(c, 2).wait_recv()
@@ -621,7 +646,7 @@
             + [jnp.zeros(((GROUPS - count) * CHUNK_OVER, LANES), bf16)],
             axis=0,
         )
-        packed[c, :, SPLIT:first] = dot(unsort[...], over).astype(bf16)
+        packed[c, :, SPLIT:first] = dot(unsort, over).astype(bf16)
         returned[c, :MAIN] = packed[c, :MAIN]
 
         @pl.loop(1, PER)
@@ -672,54 +697,65 @@
 
         @pl.when(c > 0)
         def _():
-            tokens_in[c, :, :SPLIT] = inner_sum.astype(bf16)
-            tokens_in[c, :, SPLIT:] = share_sum.astype(bf16)
-            send_plane(c).start()
+            summed[:, :SPLIT] = inner_sum
+            summed[:, SPLIT:] = share_sum
+
+        for side in (0, 1):
+            rows = slice(side * half_tokens, (side + 1) * half_tokens)
+
+            @pl.when(c == 5 + side)
+            def _():
+                send_plane(7 + side).wait_recv()
+                summed[rows] += planes[5 + side, rows].astype(f32)
+
+        @pl.when(c == 4)
+        def _():
+            send_plane(6).wait_recv()
+            summed[...] += planes[4].astype(f32)
+
+        @pl.when(c > 0)
+        def _():
+            tokens_in[c] = summed[...].astype(bf16)
+
+        for i in range(1, DEPTH):
+
+            @pl.when(c == i)
+            def _():
+                send_plane(i).start()
+                if i == 7:
+                    send_plane(8).start()
+
+    def order(p):
+        late = lax.div(p + 4, DEPTH)
+        return (1 - late) * p + late * (11 - p)
 
     pick(0)
 
     @pl.loop(0, DEPTH + 5)
     def _(t):
-        @pl.when(t < DEPTH)
-        def _():
-            @pl.loop(1, PER)
-            def _(k):
-                exchange(t, k).wait_recv()
-
-            inner[t, x] = inbox[t, :, :inner_width]
-            for i in (0, 2, 1, 3):
-                gather(t, i).start()
-
         @pl.when((t >= 1) & (t < DEPTH + 1))
         def _():
-            c = t - 1
+            c = order(t - 1)
             gather(c, 0).wait_recv()
             gather(c, 4).start()
             gather(c, 2).wait_recv()
             gather(c, 5).start()
 
-        @pl.when(t + 1 < DEPTH)
-        def _():
-            i = t + 1
-
-            @pl.when(i < DEPTH - 1)
-            def _():
-                ring(i).wait_recv()
-
-            @pl.when(i + 2 < DEPTH - 1)
-            def _():
-                ring(i + 2).start()
-
-            for side in (0, 1):
-
-                @pl.when(i == DEPTH - 3 + side)
-                def _():
-                    ring_far(side).start()
-
-                @pl.when(i == DEPTH - 1)
-                def _():
-                    ring_far(side).wait_recv()
-
+        @pl.when(t < DEPTH)
+        def _():
+            c = order(t)
+
+            @pl.loop(1, PER)
+            def _(k):
+                exchange(c, k).wait_recv()
+
+            inner[c, x] = inbox[c, :, :inner_width]
+            for i in (0, 2, 1, 3):
+                gather(c, i).start()
+
+        @pl.when((t >= DEPTH // 2) & (t + 1 < DEPTH))
+        def _():
+            i = order(t + 1)
             send_routes(i).wait_recv()
             pick(i)
 
@@ -730,14 +766,14 @@
 
         @pl.when((t >= 2) & (t < DEPTH + 2))
         def _():
-            c = t - 2
+            c = order(t - 2)
             for i in (1, 3, 4, 5):
                 gather(c, i).wait_recv()
             compute(c)
 
         @pl.when((t >= 3) & (t < DEPTH + 3))
         def _():
-            c = t - 3
+            c = order(t - 3)
             reduce(c, 0).wait_recv()
             to_right[c, :HALF_OUT] = (
                 to_right[c, :HALF_OUT].astype(f32) + far_a[c].astype(f32)
@@ -751,16 +787,40 @@
 
         @pl.when((t >= 4) & (t < DEPTH + 4))
         def _():
-            finish(t - 4)
+            finish(order(t - 4))
 
         @pl.when(t >= 5)
         def _():
-            combine(t - 5)
-
-    @pl.loop(1, DEPTH)
-    def _(i):
+            combine(order(t - 5))
+
+        @pl.when(t < 3)
+        def _():
+            for side in (0, 1):
+                i = 2 * t + 1 + side
+                ring(i).wait_recv()
+
+                @pl.when(t < 2)
+                def _():
+                    ring(i + 2).start()
+
+                @pl.when(t == 2)
+                def _():
+                    ring_far(side).start()
+
+        @pl.when(t == 3)
+        def _():
+            for side in (0, 1):
+                ring_far(side).wait_recv()
+
+        @pl.when(t < DEPTH // 2)
+        def _():
+            i = order(t + 1)
+            send_routes(i).wait_recv()
+            pick(i)
+
+    for i, slot in ((1, 1), (2, 2), (3, 3), (5, 7), (4, 0)):
         send_plane(i).wait_recv()
-        total[...] += planes[i].astype(f32)
+        total[...] += planes[slot].astype(f32)
 
     staged[...] = total[:, SPLIT:].astype(bf16)
     for i in range(3):
@@ -780,6 +840,8 @@
     @pl.loop(1, DEPTH)
     def _(i):
         send_routes(i).wait_send()
+
+    for i in range(1, DEPTH + 1):
         send_plane(i).wait_send()
 
     @pl.loop(0, DEPTH)
@@ -798,7 +860,6 @@
     tokens, wide = normed.shape
     cols = hidden.shape[1]
     ff, model_width = w_down.shape
-    order = overflow_order()
     rows = CHUNK_ROWS
     width = wide + 2 * LANES
     bf16, f32 = jnp.bfloat16, jnp.float32
@@ -809,7 +870,7 @@
     return pl.pallas_call(
         expert_kernel,
         out_shape=jax.ShapeDtypeStruct((tokens, cols), bf16),
-        in_specs=[anywhere] * 2 + [onchip] + [anywhere] * 3 + [onchip] * 2,
+        in_specs=[anywhere] * 2 + [onchip] + [anywhere] * 3,
         out_specs=onchip,
         scratch_shapes=[
             pltpu.VMEM((DEPTH, tokens, wide), bf16),
@@ -831,6 +892,7 @@
             pltpu.VMEM((DEPTH, CHUNK_MAIN, width), bf16),
             pltpu.VMEM((DEPTH, tokens, wide), bf16),
             pltpu.VMEM((tokens, wide), f32),
+            pltpu.VMEM((tokens, wide), f32),
             pltpu.VMEM((tokens, wide - SPLIT), bf16),
             pltpu.VMEM((3, tokens, cols - SPLIT), bf16),
             dma((5,)),
@@ -846,36 +908,23 @@
             dma((DEPTH, 4)),
             dma((DEPTH, PER)),
             dma((DEPTH, PER)),
-            dma((DEPTH,)),
-            dma((DEPTH,)),
+            dma((DEPTH + 1,)),
+            dma((DEPTH + 1,)),
             dma((3,)),
             dma((3,)),
         ],
         compiler_params=pltpu.CompilerParams(
             collective_id=1, has_side_effects=True, vmem_limit_bytes=60 << 20
         ),
-    )(normed, routes, hidden, w_gate, w_up, w_down, jnp.asarray(order, bf16), jnp.asarray(order.T, bf16))
+    )(normed, routes, hidden, w_gate, w_up, w_down)
 
 
 def per_device(
     attn_heads, out_proj, residual, norm_gain, route_ids, route_weights, w_gate, w_up, w_down
 ):
-    place = lax.axis_index("expert")
-    ahead_z = (route_ids % RING // 2 - place % RING // 2) % DEPTH
-    chunk = jnp.where(
-        ahead_z == 0, 0, jnp.where(ahead_z <= DEPTH // 2, 2 * ahead_z - 1, 2 * (DEPTH - ahead_z))
+    hidden, normed, routes = attention(
+        attn_heads, out_proj, residual, norm_gain, route_ids, route_weights
     )
-    ahead_y = (route_ids // RING - place // RING) % ROWS_Y
-    relative = chunk * PER + ahead_y * 2 + (route_ids - place) % 2
-    rank, weight = routing(relative, route_weights)
-    routes = jnp.concatenate(
-        [
-            rank.T.astype(jnp.float32).reshape(DEPTH, PER, -1),
-            weight.T.reshape(DEPTH, PER, -1),
-        ],
-        axis=1,
-    )
-    hidden, normed = attention(attn_heads, out_proj, residual, norm_gain)
     return experts(normed, routes, hidden, w_gate[0], w_up[0], w_down[0])
 
 

time: 287 us -> 260 us (0.906); the launches traced: 287 us -> 255 us
  Pallas kernels: 276 us -> 249 us
    pallas_call x1, Pallas kernels: 212 us -> 187 us  [experts(): pl.pallas_call(expert_kernel, out_shape=jax.ShapeDtypeStruct((tokens, col...]
    unnamed x12 -> x4, local copies, waits for them, and re-layouts: 7.18 us -> 6.25 us
where the time goes in v5:
time: 260 us; the launch traced here: 255 us
  Pallas kernels  249 us (96%)
  local copies, waits for them, and re-layouts  6.25 us (2%)
    pallas_call x1, Pallas kernels, experts(): pl.pallas_call(expert_kernel, out_shape=jax.ShapeDtypeStruct((tokens, col...  187 us
    pallas_call x1, Pallas kernels, attention(): pl.pallas_call(attention_kernel, out_shape=(jax.ShapeDtypeStruct((tokens,...  62.3 us
    unnamed x4, local copies, waits for them, and re-layouts  6.25 us

profile of v5, /device:TPU:1, one launch (start us, length us, event | category | flops | bytes accessed | tf_op | source)
XLA Modules:
  0.0 255.4 jit_solution(15564340314842121041)
XLA Ops:
  0.0 1.4 copy.11.route_ids
  1.4 1.4 copy.12.route_weights
  2.8 1.7 copy.10.proj_hbm
  4.6 62.3 %shard_map.91 = (f32[128,1024]{1,0:T(8,128)}, bf16[128,1792]{1,0:T(8,128)(2,1)}, f32[8,16,128]{2,1,0:T(8,128)}) custom-call(bf16[128,1024]{1,0:T(8,128)(2,1)} %heads_hbm.1, bf16[1024,64]{1,0:T(8,128)(2,1)} %copy.10.proj_hbm, bf16[128,4096]{1,0:T(8,128)(2,1)} %residual_hbm.1, f32[1,4096]{1,0:T(1,128)} %bitcast.7, s32[128,8]{1,0:T(8,128)} %copy.11.route_ids, ...), custom_call_target="tpu_custom_call" | custom-call | tf_op jit(solution)/shard_map/pallas_call | solution.py:314
  66.9 186.7 %shard_map.92 = bf16[128,1024]{1,0:T(8,128)(2,1)} custom-call(bf16[128,1792]{1,0:T(8,128)(2,1)} %get-tuple-element.8.normed, f32[8,16,128]{2,1,0:T(8,128)} %get-tuple-element.9.routes_in, f32[128,1024]{1,0:T(8,128)} %get-tuple-element.10.hidden, bf16[4096,384]{1,0:T(8,128)(2,1)} %bitcast.4, bf16[4096,384]{1,0:T(8,128)(2,1)} %bitcast.5, bf16[384,4096]{1,0:T(8,128)(2,1)} %bitcast.6), custom_call_target="tpu_custom_call" | custom-call | tf_op jit(solution)/shard_map/pallas_call | solution.py:870
  253.7 1.7 copy.14

commit v6 on v5

--- a/solution.py
+++ b/solution.py
@@ -29,7 +29,7 @@
     shard, sibling_shard, weight, heads, to_far, to_right, to_left, own,
     far_a, far_b, from_left, from_right, mine, arrived, residual, gain, squares,
     shared, shared_residual, shared_gain,
-    local_sem, shard_sem, zsend, zrecv, csend, crecv, hsend, hrecv, rsend, rrecv, wsem, nsend, nrecv,
+    local_sem, shard_sem, zsend, zrecv, csend, crecv, hsend, hrecv, rsend, rrecv, wsend, wrecv, nsend, nrecv,
     ssend, srecv,
 ):
     me = lax.axis_index("expert")
@@ -105,7 +105,7 @@
         )
 
     swap_shard = remote(
-        shard.at[pl.ds(pl.multiple_of((1 - core) * half, half), half)],
+        shard.at[:, pl.ds(pl.multiple_of((1 - core) * half, half), half)],
         sibling_shard,
         shard_sem.at[0],
         shard_sem.at[1],
@@ -142,24 +142,25 @@
         i = 5 * direction + s
         return remote(ref, ref, csend.at[i], crecv.at[i], (sibling, x))
 
-    width = shard.shape[1]
-    row = lax.broadcasted_iota(jnp.int32, (width, LANES), 0)
-    lane = lax.broadcasted_iota(jnp.int32, (width, LANES), 1)
-    put_own = (lane == row + width * core).astype(jnp.bfloat16)
-    put_other = (lane == row + width * (1 - core)).astype(jnp.bfloat16)
+    width = shard.shape[0]
+    row = lax.broadcasted_iota(jnp.int32, (LANES, width), 0)
+    lane = lax.broadcasted_iota(jnp.int32, (LANES, width), 1)
+    put_own = (row == lane + width * core).astype(jnp.bfloat16)
+    put_other = (row == lane + width * (1 - core)).astype(jnp.bfloat16)
     swap_shard.wait_recv()
     both = jnp.dot(
-        shard[pl.ds(pl.multiple_of(core * half, half), half), :],
         put_own,
+        shard[:, pl.ds(pl.multiple_of(core * half, half), half)],
         preferred_element_type=jnp.float32,
-    ) + jnp.dot(sibling_shard[...], put_other, preferred_element_type=jnp.float32)
+    ) + jnp.dot(put_other, sibling_shard[...], preferred_element_type=jnp.float32)
+    both = both.T
     weight[z, pl.ds(pl.multiple_of(core * half, half), half)] = both.astype(jnp.bfloat16)
     ring(0, 1).start()
     ring(1, 1).start()
     across(0, 0).start()
     square = (tokens, LANES)
-    lane = lax.broadcasted_iota(jnp.int32, square, 1)
-    earlier = jnp.where(lane < lax.broadcasted_iota(jnp.int32, square, 0), 1.0, 0.0)
+    row = lax.broadcasted_iota(jnp.int32, square, 0)
+    earlier = jnp.where(row < lax.broadcasted_iota(jnp.int32, square, 1), 1.0, 0.0)
     ids = route_ids[...]
     ahead_z = (((ids & (RING - 1)) >> 1) + depth - z) & (depth - 1)
     chunk = jnp.where(
@@ -167,20 +168,19 @@
     )
     ahead_y = ((ids >> 4) + ROWS_Y - y) & (ROWS_Y - 1)
     relative = chunk * PER + ahead_y * 2 + ((ids + 2 - core) & 1)
-    shares = route_weights[...] / jnp.sum(route_weights[...], axis=-1, keepdims=True)
+    shares = route_weights[...] / jnp.sum(route_weights[...], axis=0, keepdims=True)
     chosen = jnp.zeros(square, jnp.float32)
     scaled = jnp.zeros(square, jnp.float32)
-    for k in range(ids.shape[1]):
-        hit = lane == relative[:, k : k + 1]
+    for k in range(ids.shape[0]):
+        hit = row == relative[k : k + 1]
         chosen = jnp.where(hit, 1.0, chosen)
-        scaled = jnp.where(hit, shares[:, k : k + 1], scaled)
+        scaled = jnp.where(hit, shares[k : k + 1], scaled)
     rank = jnp.dot(
+        chosen.astype(jnp.bfloat16),
         earlier.astype(jnp.bfloat16),
-        chosen.astype(jnp.bfloat16),
         preferred_element_type=jnp.float32,
     )
-    rank = jnp.where(chosen > 0, rank, -1.0).T
-    scaled = scaled.T
+    rank = jnp.where(chosen > 0, rank, -1.0)
     for i in range(depth):
         routes_out[i, :PER] = rank[i * PER : (i + 1) * PER]
         routes_out[i, PER:] = scaled[i * PER : (i + 1) * PER]
@@ -213,36 +213,57 @@
     part = tokens // 2
 
     def reduce(i):
-        source = (to_far.at[pl.ds(0, part)], to_far.at[pl.ds(part, part)], to_right, to_left)[i]
-        landing = (far_a, far_b, from_left, from_right)[i]
-        target = (right, left, right, left)[i]
+        rows = pl.ds((0, part, part, 0, 0, part)[i], part)
+        source = (to_far, to_far, to_right, to_left, to_right, to_left)[i].at[rows]
+        landing = (
+            far_a,
+            far_b,
+            from_left.at[rows],
+            from_right.at[rows],
+            from_left.at[rows],
+            from_right.at[rows],
+        )[i]
+        target = (right, left)[i % 2]
         return remote(source, landing, rsend.at[i], rrecv.at[i], (me, target))
+
+    def exchange(i):
+        rows = pl.ds(i * part, part)
+        return remote(mine.at[rows], arrived.at[rows], wsend.at[i], wrecv.at[i], partner)
 
     to_far[...] = partial(far).astype(jnp.bfloat16)
     reduce(0).start()
     reduce(1).start()
     via_right = partial(right)
-    reduce(0).wait_recv()
-    to_right[:part] = (via_right[:part] + far_a[...].astype(jnp.float32)).astype(jnp.bfloat16)
     to_right[part:] = via_right[part:].astype(jnp.bfloat16)
     reduce(2).start()
     via_left = partial(left)
+    to_left[:part] = via_left[:part].astype(jnp.bfloat16)
+    reduce(3).start()
+    reduce(0).wait_recv()
+    to_right[:part] = (via_right[:part] + far_a[...].astype(jnp.float32)).astype(jnp.bfloat16)
+    reduce(4).start()
     reduce(1).wait_recv()
-    to_left[:part] = via_left[:part].astype(jnp.bfloat16)
     to_left[part:] = (via_left[part:] + far_b[...].astype(jnp.float32)).astype(jnp.bfloat16)
-    reduce(3).start()
+    reduce(5).start()
     own[...] = partial(x)
-    reduce(2).wait_recv()
-    reduce(3).wait_recv()
-    mine[...] = (
-        own[...] + from_left[...].astype(jnp.float32) + from_right[...].astype(jnp.float32)
-    ).astype(jnp.bfloat16)
-    exchange = remote(mine, arrived, wsem.at[0], wsem.at[1], partner)
+    for i in range(2):
+        rows = slice(i * part, (i + 1) * part)
+        reduce((4, 2)[i]).wait_recv()
+        reduce((3, 5)[i]).wait_recv()
+        mine[rows] = (
+            own[rows]
+            + from_left[rows].astype(jnp.float32)
+            + from_right[rows].astype(jnp.float32)
+        ).astype(jnp.bfloat16)
+
+        @pl.when(x != y)
+        def _():
+            exchange(i).start()
 
     @pl.when(x != y)
     def _():
-        exchange.start()
-        exchange.wait_recv()
+        exchange(0).wait_recv()
+        exchange(1).wait_recv()
 
     @pl.when(x == y)
     def _():
@@ -287,7 +308,8 @@
 
     @pl.when(x != y)
     def _():
-        exchange.wait_send()
+        exchange(0).wait_send()
+        exchange(1).wait_send()
 
     swap_shard.wait_send()
     for i in range(3):
@@ -299,7 +321,7 @@
     for s in range(1, depth // 2 + 1):
         for direction in (0, 1):
             ring(direction, s).wait_send()
-    for i in range(4):
+    for i in range(6):
         reduce(i).wait_send()
 
 
@@ -322,7 +344,7 @@
         out_specs=(onchip, onchip, onchip),
         scratch_shapes=[
             pltpu.VMEM(out_proj.shape, bf16),
-            pltpu.VMEM((depth // 2, out_proj.shape[1]), bf16),
+            pltpu.VMEM((out_proj.shape[0], depth // 2), bf16),
             pltpu.VMEM((RING // 2, depth, LANES), bf16),
             pltpu.VMEM((ROWS_Y, tokens, depth), bf16),
             block,
@@ -349,8 +371,9 @@
             dma((10,)),
             dma((3,)),
             dma((3,)),
-            dma((4,)),
-            dma((4,)),
+            dma((6,)),
+            dma((6,)),
+            dma((2,)),
             dma((2,)),
             dma((3,)),
             dma((3,)),
@@ -502,11 +525,18 @@
     head, tail = pl.ds(0, HALF_OUT), pl.ds(HALF_OUT, CHUNK_ROWS - HALF_OUT)
 
     def reduce(c, i):
-        source = (to_far.at[c, head], to_far.at[c, tail], to_right.at[c], to_left.at[c])[i]
-        landing = (far_a.at[c], far_b.at[c], from_left.at[c], from_right.at[c])[i]
-        return remote(
-            source, landing, rsend.at[c, i], rrecv.at[c, i], (me, (right, left, right, left)[i])
-        )
+        rows = (head, tail, tail, head, head, tail)[i]
+        source = (to_far, to_far, to_right, to_left, to_right, to_left)[i].at[c, rows]
+        landing = (
+            far_a.at[c],
+            far_b.at[c],
+            from_left.at[c, rows],
+            from_right.at[c, rows],
+            from_left.at[c, rows],
+            from_right.at[c, rows],
+        )[i]
+        target = (right, left)[i % 2]
+        return remote(source, landing, rsend.at[c, i], rrecv.at[c, i], (me, target))
 
     half_tokens = tokens_in.shape[1] // 2
 
@@ -620,9 +650,11 @@
         keep_share(far, value)
         value = project(act, right)
         to_right[c] = value[:, :SPLIT].astype(bf16)
+        reduce(c, 2).start()
         keep_share(right, value)
         value = project(act, left)
         to_left[c] = value[:, :SPLIT].astype(bf16)
+        reduce(c, 3).start()
         keep_share(left, value)
         value = project(act, x)
         own[c] = value[:, :SPLIT]
@@ -634,8 +666,8 @@
         packed[c, :, last:] = dot(unsort, over).astype(bf16)
 
     def finish(c):
-        reduce(c, 2).wait_recv()
-        reduce(c, 3).wait_recv()
+        for i in (2, 3, 4, 5):
+            reduce(c, i).wait_recv()
         value = (
             own[c] + from_left[c].astype(f32) + from_right[c].astype(f32)
         ).astype(bf16)
@@ -778,12 +810,12 @@
             to_right[c, :HALF_OUT] = (
                 to_right[c, :HALF_OUT].astype(f32) + far_a[c].astype(f32)
             ).astype(bf16)
-            reduce(c, 2).start()
+            reduce(c, 4).start()
             reduce(c, 1).wait_recv()
             to_left[c, HALF_OUT:] = (
                 to_left[c, HALF_OUT:].astype(f32) + far_b[c].astype(f32)
             ).astype(bf16)
-            reduce(c, 3).start()
+            reduce(c, 5).start()
 
         @pl.when((t >= 4) & (t < DEPTH + 4))
         def _():
@@ -825,12 +857,12 @@
     staged[...] = total[:, SPLIT:].astype(bf16)
     for i in range(3):
         send_quarter(i).start()
-    out[:, :SPLIT] = (hidden[:, :SPLIT] + total[:, :SPLIT]).astype(bf16)
+    out[:, :SPLIT] = hidden[:, :SPLIT] + total[:, :SPLIT]
     mixture = total[:, pl.ds(pl.multiple_of(SPLIT + x * share, share), share)]
     for i in range(3):
         send_quarter(i).wait_recv()
         mixture += quarters[i].astype(f32)
-    out[:, SPLIT:] = (hidden[:, SPLIT:] + mixture).astype(bf16)
+    out[:, SPLIT:] = hidden[:, SPLIT:] + mixture
 
     for i in (1, 2):
         ring(i, 0).wait_send()
@@ -848,7 +880,6 @@
     def _(c):
         for i in range(6):
             gather(c, i).wait_send()
-        for i in range(4):
             reduce(c, i).wait_send()
 
         @pl.loop(1, PER)
@@ -869,7 +900,7 @@
     moved = pltpu.VMEM((DEPTH, rows, SPLIT), bf16)
     return pl.pallas_call(
         expert_kernel,
-        out_shape=jax.ShapeDtypeStruct((tokens, cols), bf16),
+        out_shape=jax.ShapeDtypeStruct((tokens, cols), f32),
         in_specs=[anywhere] * 2 + [onchip] + [anywhere] * 3,
         out_specs=onchip,
         scratch_shapes=[
@@ -904,8 +935,8 @@
             dma((DEPTH, PER)),
             dma((DEPTH, 6)),
             dma((DEPTH, 6)),
-            dma((DEPTH, 4)),
-            dma((DEPTH, 4)),
+            dma((DEPTH, 6)),
+            dma((DEPTH, 6)),
             dma((DEPTH, PER)),
             dma((DEPTH, PER)),
             dma((DEPTH + 1,)),
@@ -923,9 +954,10 @@
     attn_heads, out_proj, residual, norm_gain, route_ids, route_weights, w_gate, w_up, w_down
 ):
     hidden, normed, routes = attention(
-        attn_heads, out_proj, residual, norm_gain, route_ids, route_weights
+        attn_heads, out_proj.T, residual, norm_gain, route_ids.T, route_weights.T
     )
-    return experts(normed, routes, hidden, w_gate[0], w_up[0], w_down[0])
+    layer_out = experts(normed, routes, hidden, w_gate[0], w_up[0], w_down[0])
+    return layer_out.astype(jnp.bfloat16)
 
 
 def solution(mesh):

time: 260 us -> 255 us (0.981)
  local copies, waits for them, and re-layouts: 6.25 us -> 0 us
    unnamed x4 -> x0, local copies, waits for them, and re-layouts: 6.25 us -> none
where the time goes in v6:
time: 255 us; the launch traced here: 253 us
  Pallas kernels  251 us (98%)
    pallas_call x1, Pallas kernels, experts(): pl.pallas_call(expert_kernel, out_shape=jax.ShapeDtypeStruct((tokens, col...  188 us
    pallas_call x1, Pallas kernels, attention(): pl.pallas_call(attention_kernel, out_shape=(jax.ShapeDtypeStruct((tokens,...  62.5 us

profile of v6, /device:TPU:1, one launch (start us, length us, event | category | flops | bytes accessed | tf_op | source)
XLA Modules:
  0.0 252.5 jit_solution(7941752594929934036)
XLA Ops:
  0.0 62.5 %shard_map.91 = (f32[128,1024]{1,0:T(8,128)}, bf16[128,1792]{1,0:T(8,128)(2,1)}, f32[8,16,128]{2,1,0:T(8,128)}) custom-call(bf16[128,1024]{1,0:T(8,128)(2,1)} %heads_hbm.1, bf16[64,1024]{1,0:T(8,128)(2,1)} %bitcast.10, bf16[128,4096]{1,0:T(8,128)(2,1)} %residual_hbm.1, f32[1,4096]{1,0:T(1,128)} %bitcast.11, s32[8,128]{1,0:T(8,128)} %bitcast.12, ...), custom_call_target="tpu_custom_call" | custom-call | tf_op jit(solution)/shard_map/pallas_call | solution.py:336
  62.5 188.3 %shard_map.92 = f32[128,1024]{1,0:T(8,128)} custom-call(bf16[128,1792]{1,0:T(8,128)(2,1)} %get-tuple-element.8.normed, f32[8,16,128]{2,1,0:T(8,128)} %get-tuple-element.9.routes_in, f32[128,1024]{1,0:T(8,128)} %get-tuple-element.10.hidden, bf16[4096,384]{1,0:T(8,128)(2,1)} %bitcast.7, bf16[4096,384]{1,0:T(8,128)(2,1)} %bitcast.8, bf16[384,4096]{1,0:T(8,128)(2,1)} %bitcast.9), custom_call_target="tpu_custom_call" | custom-call | tf_op jit(solution)/shard_map/pallas_call | solution.py:901
  250.8 1.8 convert_element_type.3

commit v7 on v6

--- a/solution.py
+++ b/solution.py
@@ -597,7 +597,7 @@
 
         @pl.loop(1, PER)
         def _(k):
-            exchange(i, k).start()
+            exchange(i, 1 + lax.rem(k + 2, PER - 1)).start()
 
     def project(act, quarter):
         columns = pl.ds(pl.multiple_of(quarter * cols, cols), cols)
@@ -683,7 +683,7 @@
 
         @pl.loop(1, PER)
         def _(k):
-            give_back(c, k).start()
+            give_back(c, 1 + lax.rem(k + 2, PER - 1)).start()
 
     def combine(c):
         @pl.loop(1, PER)

time: 255 us -> 254 us (level)
  no operation moved by 1% of the time
where the time goes in v7:
time: 254 us; the launch traced here: 253 us
  Pallas kernels  251 us (99%)
    pallas_call x1, Pallas kernels, experts(): pl.pallas_call(expert_kernel, out_shape=jax.ShapeDtypeStruct((tokens, col...  189 us
    pallas_call x1, Pallas kernels, attention(): pl.pallas_call(attention_kernel, out_shape=(jax.ShapeDtypeStruct((tokens,...  62.5 us

profile of v7, /device:TPU:1, one launch (start us, length us, event | category | flops | bytes accessed | tf_op | source)
XLA Modules:
  0.0 253.1 jit_solution(8822832878234463582)
XLA Ops:
  0.0 62.5 %shard_map.91 = (f32[128,1024]{1,0:T(8,128)}, bf16[128,1792]{1,0:T(8,128)(2,1)}, f32[8,16,128]{2,1,0:T(8,128)}) custom-call(bf16[128,1024]{1,0:T(8,128)(2,1)} %heads_hbm.1, bf16[64,1024]{1,0:T(8,128)(2,1)} %bitcast.10, bf16[128,4096]{1,0:T(8,128)(2,1)} %residual_hbm.1, f32[1,4096]{1,0:T(1,128)} %bitcast.11, s32[8,128]{1,0:T(8,128)} %bitcast.12, ...), custom_call_target="tpu_custom_call" | custom-call | tf_op jit(solution)/shard_map/pallas_call | solution.py:336
  62.5 188.8 %shard_map.92 = f32[128,1024]{1,0:T(8,128)} custom-call(bf16[128,1792]{1,0:T(8,128)(2,1)} %get-tuple-element.8.normed, f32[8,16,128]{2,1,0:T(8,128)} %get-tuple-element.9.routes_in, f32[128,1024]{1,0:T(8,128)} %get-tuple-element.10.hidden, bf16[4096,384]{1,0:T(8,128)(2,1)} %bitcast.7, bf16[4096,384]{1,0:T(8,128)(2,1)} %bitcast.8, bf16[384,4096]{1,0:T(8,128)(2,1)} %bitcast.9), custom_call_target="tpu_custom_call" | custom-call | tf_op jit(solution)/shard_map/pallas_call | solution.py:901
  251.3 1.8 convert_element_type.3
